TPU v7x, 32 devices: a whole 2x2x4 slice. The times are simulated.
32 devices in a mesh: row: 8 (over z, core), col: 4 (over y, x).
Axes of the slice: x: 2, y: 2, z: 4, core: 2. Of those that a mesh axis runs over, the one named last changes fastest.
Arguments:
- eigenvectors: float32 [4096, 512], P('row', 'col'), may hold values from -6 to 6
- aligned_vectors: float32 [2, 4096, 256], P(None, 'row', 'col'), may hold values from -0.3 to 1, as said below
- straddle_vectors: float32 [2, 4096, 256], P(None, 'row', 'col'), may hold values from -0.3 to 1, as said below
Outputs:
- transformed: float32 [4096, 512], P('row', 'col')
Inputs may be any that keep to these rules, and one draw needn't show every extreme that they name: `aligned_vectors`: within each block of 512 rows, column i is 1 in the block's row i and 0 in the rows above it. `straddle_vectors`: within each straddling block of the steps, column i is 1 in the block's row i and 0 in the rows above it.
All inputs are finite; a program needn't handle non-finite values.
Results may differ from a plain program's by a relative error of at most 0.00027.
Values sent between devices are 32-bit elements; how exact they have to be, the bound alone decides.
No kernel may reach another device: no remote copies, remote signals or barrier semaphores. Data moves between devices by JAX's collectives and lax.ppermute only.
A program may use at most 128 MiB of HBM per device.

v0:
```python
import functools

import jax
import jax.numpy as jnp
from jax import lax
from jax.experimental import pallas as pl
from jax.experimental.pallas import tpu as pltpu
from jax.sharding import PartitionSpec as P

F32 = jnp.float32
BF16 = jnp.bfloat16
BASE_BLOCK = 32


def split(value):
    high = value.astype(BF16)
    return high, (value - high.astype(F32)).astype(BF16)


def raw_dot(left, right, transposed):
    dims = (((1,), (1 if transposed else 0,)), ((), ()))
    return lax.dot_general(left, right, dims, preferred_element_type=F32)


def product(left, right, transposed=False):
    left = left if isinstance(left, tuple) else split(left)
    right = right if isinstance(right, tuple) else split(right)
    return (
        raw_dot(left[0], right[0], transposed)
        + raw_dot(left[0], right[1], transposed)
        + raw_dot(left[1], right[0], transposed)
    )


def cut(pair, rows=slice(None), lanes=slice(None)):
    return pair[0][rows, lanes], pair[1][rows, lanes]


def lower_inverses(grams):
    order = grams[0].shape[0]
    base = min(BASE_BLOCK, order)
    rows = lax.broadcasted_iota(jnp.int32, (order, order), 0)
    lanes = lax.broadcasted_iota(jnp.int32, (order, order), 1)
    identity = jnp.where(rows == lanes, 1.0, 0.0).astype(F32)
    strict = [jnp.where(rows > lanes, gram, 0.0) for gram in grams]
    across = [2.0 / jnp.sum(gram * identity, axis=0, keepdims=True) for gram in grams]
    along = [2.0 / jnp.sum(gram * identity, axis=1, keepdims=True) for gram in grams]
    same = rows // base == lanes // base
    nilpotent = [jnp.where(same, low * scale, 0.0) for low, scale in zip(strict, across)]
    result = [identity - value for value in nilpotent]
    powered = [split(value) for value in nilpotent]
    for level in range((base - 1).bit_length() - 1):
        squares = [product(value, value) for value in powered]
        powered = [split(value) for value in squares]
        result = [
            now + product(now, value) for now, value in zip(result, powered)
        ]
    result = [now * scale for now, scale in zip(result, along)]
    size = base
    while size < order:
        here = (rows // (2 * size) == lanes // (2 * size)) & (rows // size != lanes // size)
        parts = [split(now) for now in result]
        inner = [
            product(part, jnp.where(here, low, 0.0)) for part, low in zip(parts, strict)
        ]
        result = [
            now - product(value, part) for now, value, part in zip(result, inner, parts)
        ]
        size *= 2
    return result


def place(pieces, index_ref, first, target, width):
    for at, (piece, sweeps) in enumerate(pieces):
        start = pl.multiple_of(index_ref[first + at] * width, width)
        for sweep, source in sweeps:
            target[sweep, pl.ds(start, width), :] = piece[source]


def gram_kernel(layout, width, half, index_ref, *refs):
    count = len(layout)
    pieces = [(refs[at], layout[at]) for at in range(count)]
    matrix_ref, wide_ref, inner_ref, outer_ref = refs[count:]
    place(pieces, index_ref, 4, wide_ref, width)
    even = index_ref[0] == 0
    sweeps = wide_ref.shape[0]
    for sweep in range(sweeps):
        whole = split(wide_ref[sweep])
        below, above = cut(whole, lanes=slice(0, half)), cut(whole, lanes=slice(half, None))
        gram_below, gram_above = product(below, below, True), product(above, above, True)
        at = slice(sweep * half, (sweep + 1) * half)
        inner_ref[at, :] = jnp.where(even, gram_above, gram_below)
        outer_ref[at, :] = jnp.where(even, gram_below, gram_above)
        if sweep == 0:
            lower_rows = jnp.transpose(matrix_ref[half:, :])
            first = product(lower_rows, above, True)
            inner_ref[sweeps * half :, :] = first
            outer_ref[sweeps * half :, :] = first


def local_kernel(layout, width, half, index_ref, *refs):
    count = len(layout)
    pieces = [(refs[at], layout[at]) for at in range(count)]
    (
        matrix_ref, straddle_ref, inner_ref, inner_got_ref, outer_ref, outer_got_ref,
        wide_ref, step_ref, up_ref, now_ref, coeff_ref, factor_ref, square_ref,
    ) = refs[count:]
    place(pieces, index_ref, 4, wide_ref, width)
    parity = index_ref[0]
    even = parity == 0
    outside = jnp.where(index_ref[1] == 0, 1.0, 0.0)
    columns = matrix_ref.shape[1]
    grams = []
    for sweep in range(2):
        at = slice(sweep * half, (sweep + 1) * half)
        aligned = split(wide_ref[sweep])
        grams.append(inner_ref[at, :] + inner_got_ref[at, :])
        grams.append(outer_ref[at, :] + outside * outer_got_ref[at, :])
        grams.append(product(aligned, aligned, True))
    factors = lower_inverses(grams)
    for sweep in range(2):
        square_ref[sweep, parity] = factors[3 * sweep]
        square_ref[sweep, 1 - parity] = factors[3 * sweep + 1]
    top = slice(2 * half, 2 * half + columns)
    own_first = inner_ref[top, :]
    got_first = jnp.where(even, outside * outer_got_ref[top, :], inner_got_ref[top, :])

    current = jnp.transpose(matrix_ref[...])
    upper, lower = current[:, :half], current[:, half:]
    blank = jnp.zeros((half, half), F32)

    def pieces_of(sweep):
        straddle, aligned = split(straddle_ref[sweep]), split(wide_ref[sweep])
        return (
            cut(straddle, lanes=slice(0, half)), cut(straddle, lanes=slice(half, None)),
            cut(aligned, lanes=slice(0, half)), cut(aligned, lanes=slice(half, None)),
        )

    below, above, aligned_up, aligned_low = pieces_of(0)
    factor_above, factor_below = split(square_ref[0, 0]), split(square_ref[0, 1])
    factor_aligned = split(factors[2])
    through = split(product(above, aligned_low, True))
    onward = split(product(aligned_up, below, True))
    seen = product(upper, aligned_up, True) + product(lower, aligned_low, True)
    raw = product(upper, below, True)
    outer = jnp.concatenate([product(own_first, factor_above), square_ref[0, 0]], axis=0)
    outer_pair = split(outer)
    inside = jnp.concatenate([seen, blank], axis=0) - product(outer_pair, through)
    coeffs = split(product(inside, factor_aligned))
    carry = jnp.concatenate([raw, blank], axis=0) - product(coeffs, onward)
    step_ref[0:half, :] = carry[columns:]
    step_ref[3 * half : 3 * half + columns, :] = carry[:columns]
    back = split(
        product(
            jnp.concatenate([carry[:columns] + got_first, carry[columns:]], axis=0), factor_below
        )
    )
    upper = (
        jnp.concatenate([upper, blank], axis=0) - product(coeffs, aligned_up) - product(back, below)
    )
    lower = (
        jnp.concatenate([lower, blank], axis=0)
        - product(outer_pair, above)
        - product(coeffs, aligned_low)
    )
    now_ref[:, :half] = upper
    now_ref[:, half:] = lower

    below, above, aligned_up, aligned_low = pieces_of(1)
    factor_above = split(square_ref[1, 0])
    factor_aligned = split(factors[5])
    factor_ref[...] = square_ref[1, 1]
    through = split(product(above, aligned_low, True))
    onward = split(product(aligned_up, below, True))
    upper, lower = split(upper), split(lower)
    first = product(lower, above, True)
    up_ref[...] = first
    seen = product(upper, aligned_up, True) + product(lower, aligned_low, True)
    raw = product(upper, below, True)
    outer = jnp.concatenate([product(first, factor_above), square_ref[1, 0]], axis=0)
    inside = jnp.concatenate([seen, blank], axis=0) - product(outer, through)
    coeffs = product(inside, factor_aligned)
    carry = jnp.concatenate([raw, blank], axis=0) - product(coeffs, onward)
    coeff_ref[:, 0:half] = outer
    coeff_ref[:, half : 2 * half] = coeffs
    coeff_ref[:, 2 * half :] = carry
    step_ref[half : 2 * half, :] = carry[columns : columns + half]
    step_ref[2 * half : 3 * half, :] = carry[columns + half :]
    step_ref[3 * half + columns :, :] = carry[:columns]


def compose_kernel(half, index_ref, own_ref, got_ref, chain_ref, start_ref, both_ref):
    parity = index_ref[0]
    both_ref[parity] = own_ref[...]
    both_ref[1 - parity] = got_ref[...]
    columns = start_ref.shape[0] * 2
    part = columns // 2

    def block(core, at):
        return split(both_ref[core, at * half : (at + 1) * half, :])

    even0, even_mix, even1 = (block(0, at) for at in range(3))
    odd0, odd_mix, odd1 = (block(1, at) for at in range(3))
    chain_ref[0:half, :] = product(odd0, even0)
    chain_ref[half : 2 * half, :] = product(odd0, even_mix) + product(odd_mix, even1)
    chain_ref[2 * half :, :] = product(odd1, even1)

    def rows(core, sweep):
        start = pl.multiple_of(3 * half + sweep * columns + parity * part, 8)
        return both_ref[core, pl.ds(start, part), :]

    odd_first = split(rows(1, 0))
    start_ref[:, :half] = rows(0, 0) + product(odd_first, even0)
    start_ref[:, half:] = (
        rows(0, 1) + product(odd_first, even_mix) + product(rows(1, 1), even1)
    )


def hop_kernel(half, start_ref, chain_ref, got_ref, out_ref):
    zero, one = split(got_ref[:, :half]), split(got_ref[:, half:])
    out_ref[:, :half] = start_ref[:, :half] + product(zero, chain_ref[0:half, :])
    out_ref[:, half:] = (
        start_ref[:, half:]
        + product(zero, chain_ref[half : 2 * half, :])
        + product(one, chain_ref[2 * half :, :])
    )


def response_kernel(
    half, index_ref, own_ref, got_ref, up_ref, now_ref, coeff_ref, factor_ref, straddle_ref, wide_ref,
    base_ref, reply_ref,
):
    columns = base_ref.shape[0]
    keep = jnp.where(index_ref[2] == 0, 1.0, 0.0)
    given = split(keep * up_ref[columns:, :])
    first = jnp.concatenate(
        [own_ref[3 * half : 3 * half + columns, :], own_ref[0:half, :]], axis=0
    )
    offset = product(first, given)
    offset = jnp.concatenate(
        [offset[:columns] + keep * up_ref[:columns, :], offset[columns:]], axis=0
    )
    reach = columns + half
    carry = coeff_ref[:, 2 * half :]
    summed = jnp.concatenate([carry[:reach] + offset, carry[reach:]], axis=0)
    back = split(product(summed, factor_ref[...]))
    outer, coeffs = split(coeff_ref[:, 0:half]), split(coeff_ref[:, half : 2 * half])
    straddle, aligned = split(straddle_ref[0]), split(wide_ref[0])
    change_up = product(coeffs, cut(aligned, lanes=slice(0, half))) + product(
        back, cut(straddle, lanes=slice(0, half))
    )
    change_low = product(outer, cut(straddle, lanes=slice(half, None))) + product(
        coeffs, cut(aligned, lanes=slice(half, None))
    )
    change = jnp.concatenate([change_up, change_low], axis=1)
    base = now_ref[:columns, :] - change[:columns]
    middle = now_ref[columns:, :] - change[columns:reach]
    last = -change[reach:]

    @pl.when(index_ref[0] != 0)
    def _():
        base_ref[...] = base
        reply_ref[0:half, :] = middle
        reply_ref[half:, :] = last

    @pl.when(index_ref[0] == 0)
    def _():
        middle_pair, last_pair = split(middle), split(last)
        zero = split(
            jnp.concatenate([got_ref[3 * half : 3 * half + columns, :], got_ref[0:half, :]], axis=0)
        )
        one = split(
            jnp.concatenate([got_ref[3 * half + columns :, :], got_ref[half : 3 * half, :]], axis=0)
        )
        after_zero = product(zero, middle_pair)
        after_one = product(one, last_pair)
        base_ref[...] = base + after_zero[:columns] + after_one[:columns]
        reply_ref[0:half, :] = after_zero[columns:] + after_one[columns:reach]
        reply_ref[half:, :] = after_one[reach:]


def final_kernel(index_ref, own_ref, got_ref, base_ref, reply_ref, out_ref, carry_ref):
    parity = index_ref[0]
    carry_ref[parity] = own_ref[...]
    carry_ref[1 - parity] = got_ref[...]
    carry = jnp.concatenate([carry_ref[0], carry_ref[1]], axis=0)
    out_ref[...] = jnp.transpose(base_ref[...] + product(carry, reply_ref[...]))


def call(body, outs, *operands, scratch=(), flops=0):
    space = pl.BlockSpec(memory_space=pltpu.VMEM)
    first = [pl.BlockSpec(memory_space=pltpu.SMEM)] if operands[0].dtype == jnp.int32 else [space]
    shapes = [jax.ShapeDtypeStruct(shape, F32) for shape in outs]
    moved = sum(4 * operand.size for operand in operands) + sum(4 * shape.size for shape in shapes)
    return pl.pallas_call(
        body,
        out_shape=shapes,
        in_specs=first + [space] * (len(operands) - 1),
        out_specs=[space] * len(shapes),
        scratch_shapes=list(scratch),
        cost_estimate=pl.CostEstimate(flops=flops, bytes_accessed=moved, transcendentals=0),
    )(*operands)


def gathered(shard, axis):
    count = lax.axis_size(axis)
    me = lax.axis_index(axis)
    every = ((0, 0), (1, 1))
    if count == 4:
        swaps = [[(i, i ^ mask) for i in range(count)] for mask in (1, 2)]
        near = lax.ppermute(shard, axis, swaps[0])
        side = lax.ppermute(shard, axis, swaps[1])
        far_first = lax.ppermute(side[0:1], axis, swaps[0])
        far_second = lax.ppermute(near[1:2], axis, swaps[1])
        arrays = [shard, near, side, far_first, far_second]
        places = [me, me ^ 1, me ^ 2, me ^ 3, me ^ 3]
        return arrays, places, [every, every, every, ((0, 0),), ((1, 0),)]
    arrays, places, layout = [shard], [me], [every]
    for step in range(1, count):
        route = [((i + step) % count, i) for i in range(count)]
        arrays.append(lax.ppermute(shard, axis, route))
        places.append((me + step) % count)
        layout.append(every)
    return arrays, places, layout


def on_device(eigenvectors, aligned_vectors, straddle_vectors):
    aligned = jnp.swapaxes(aligned_vectors, 1, 2)
    straddle = jnp.swapaxes(straddle_vectors, 1, 2)
    sweeps, width, span = aligned.shape
    half = span // 2
    columns = eigenvectors.shape[1]
    part = columns // 2
    rows = lax.axis_size("row")
    row = lax.axis_index("row")
    chips = rows // 2

    straddle_parts, places, layout = gathered(straddle, "col")
    aligned_parts, _, _ = gathered(aligned, "col")
    parity = row % 2
    outside = jnp.where(parity == 0, row == 0, row == rows - 1)
    index = jnp.stack(
        [parity, outside.astype(jnp.int32), (row == 0).astype(jnp.int32), row]
        + [jnp.asarray(place, jnp.int32) for place in places]
    ).astype(jnp.int32)
    unit = 2 * half * half * half * 3

    wide_straddle, inner, outer = call(
        functools.partial(gram_kernel, layout, width, half),
        [(sweeps, half, span), (sweeps * half + columns, half), (sweeps * half + columns, half)],
        index, *straddle_parts, eigenvectors, flops=5 * unit,
    )
    inside_route = [(i, i ^ 1) for i in range(rows)]
    outside_route = [(i, (i - 1 if i % 2 == 0 else i + 1) % rows) for i in range(rows)]
    inner_got = lax.ppermute(inner, "row", inside_route)
    outer_got = lax.ppermute(outer, "row", outside_route)
    reach = columns + half
    wide_aligned, step, up, now, coeff, factor, _ = call(
        functools.partial(local_kernel, layout, width, half),
        [
            (sweeps, half, span), (3 * half + 2 * columns, half), (reach, half), (reach, span),
            (reach + half, 3 * half), (half, half), (2, 2, half, half),
        ],
        index, *aligned_parts, eigenvectors, wide_straddle, inner, inner_got, outer, outer_got,
        flops=140 * unit,
    )
    step_got = lax.ppermute(step, "row", inside_route)
    up_got = lax.ppermute(up, "row", [(i, i + 1) for i in range(rows - 1)])
    chain, start = call(
        functools.partial(compose_kernel, half),
        [(3 * half, half), (part, span)],
        index, step, step_got, scratch=[pltpu.VMEM((2,) + step.shape, F32)], flops=6 * unit,
    )
    down = [(i, i - 2) for i in range(2, rows)]
    carry = start
    for hop in range(chips - 1):
        got = lax.ppermute(carry, "row", down)
        if hop < chips - 2:
            (carry,) = call(
                functools.partial(hop_kernel, half), [(part, span)], start, chain, got, flops=unit
            )
    if chips == 1:
        got = jnp.zeros_like(start)
    base, reply = call(
        functools.partial(response_kernel, half),
        [(columns, span), (span, span)],
        index, step, step_got, up_got, now, coeff, factor, wide_straddle[1:], wide_aligned[1:],
        flops=30 * unit,
    )
    other = lax.ppermute(got, "row", inside_route)
    (result,) = call(
        final_kernel, [(span, columns)], index, got, other, base, reply,
        scratch=[pltpu.VMEM((2, part, span), F32)], flops=4 * unit,
    )
    return result


def solution(mesh):
    placed = (P("row", "col"), P(None, "row", "col"), P(None, "row", "col"))
    return jax.shard_map(
        on_device, mesh=mesh, in_specs=placed, out_specs=P("row", "col"), check_vma=False
    )
```

profile of v0, /device:TPU:0, one launch (start us, length us, event | category | flops | bytes accessed | tf_op | source)
XLA Modules:
  0.0 104.2 jit_solution(11852563517804158169)
XLA Ops:
  0.0 3.0 %collective-permute-start.5 = (f32[2,64,512]{2,1,0:T(8,128)}, f32[2,64,512]{2,1,0:T(8,128)S(1)}, u32[]{:S(2)}, u32[]{:S(2)}) collective-permute-start(f32[2,64,512]{2,1,0:T(8,128)} %bitcast.10), channel_id=1, source_target_pairs={{0,2},{1,3},{2,0},{3,1},{4,6},{5,7},{6,4},{7,5},{8,10},{9,11},{10,... | collective-permute-start | bytes 786440 | tf_op jit(solution)/shard_map/ppermute | solution.py:312
  3.0 1.5 %collective-permute-start.4 = (f32[2,64,512]{2,1,0:T(8,128)}, f32[2,64,512]{2,1,0:T(8,128)S(1)}, u32[]{:S(2)}, u32[]{:S(2)}) collective-permute-start(f32[2,64,512]{2,1,0:T(8,128)} %bitcast.11), channel_id=1, source_target_pairs={{0,1},{1,0},{2,3},{3,2},{4,5},{5,4},{6,7},{7,6},{8,9},{9,8},{10,11... | collective-permute-start | bytes 786440 | tf_op jit(solution)/shard_map/ppermute | solution.py:311
  4.5 5.0 %collective-permute-done.5.refs_2_ = f32[2,64,512]{2,1,0:T(8,128)S(1)} collective-permute-done((f32[2,64,512]{2,1,0:T(8,128)}, f32[2,64,512]{2,1,0:T(8,128)S(1)}, u32[]{:S(2)}, u32[]{:S(2)}) %collective-permute-start.5) | collective-permute-done | bytes 262176 | tf_op jit(solution)/shard_map/ppermute | solution.py:312
  9.5 1.8 %collective-permute-start.6 = (f32[1,64,512]{2,1,0:T(8,128)S(1)}, f32[1,64,512]{2,1,0:T(8,128)S(1)}, u32[]{:S(2)}, u32[]{:S(2)}) collective-permute-start(f32[1,64,512]{2,1,0:T(8,128)S(1)} %slice.26), channel_id=1, source_target_pairs={{0,1},{1,0},{2,3},{3,2},{4,5},{5,4},{6,7},{7,6},{8,9},{9,8},{10,11... | collective-permute-start | bytes 393224 | tf_op jit(solution)/shard_map/ppermute | solution.py:313
  11.3 1.6 %collective-permute-start.7 = (f32[1,64,512]{2,1,0:T(8,128)S(1)}, f32[1,64,512]{2,1,0:T(8,128)S(1)}, u32[]{:S(2)}, u32[]{:S(2)}) collective-permute-start(f32[1,64,512]{2,1,0:T(8,128)S(1)} %slice.27), channel_id=1, source_target_pairs={{0,2},{1,3},{2,0},{3,1},{4,6},{5,7},{6,4},{7,5},{8,10},{9,11},{10,... | collective-permute-start | bytes 393224 | tf_op jit(solution)/shard_map/ppermute | solution.py:314
  13.6 1.0 collective-permute-done.6.refs_3_
  14.6 1.8 %collective-permute-done.7.refs_4_ = f32[1,64,512]{2,1,0:T(8,128)S(1)} collective-permute-done((f32[1,64,512]{2,1,0:T(8,128)S(1)}, f32[1,64,512]{2,1,0:T(8,128)S(1)}, u32[]{:S(2)}, u32[]{:S(2)}) %collective-permute-start.7) | collective-permute-done | bytes 131104 | tf_op jit(solution)/shard_map/ppermute | solution.py:314
  17.0 3.3 %shard_map.37 = (f32[2,256,512]{2,1,0:T(8,128)}, f32[640,256]{1,0:T(8,128)}, f32[640,256]{1,0:T(8,128)}) custom-call(s32[9]{0:T(128)} %stack.44.index_ref, f32[2,64,512]{2,1,0:T(8,128)} %bitcast.12, f32[2,64,512]{2,1,0:T(8,128)} %copy-done.7, f32[2,64,512]{2,1,0:T(8,128)} %copy-done.6, f32[1,64,512]{2,1,0:T(8,128)} %copy-done.16, f32[1,64,512]{2,1,0:T(8,128)} %copy-done.17, ...), custom_call_target="tpu_custom_call" | custom-call | flops 503316480 | bytes 3670052 | tf_op jit(solution)/shard_map/pallas_call | solution.py:295
  20.3 3.7 %collective-permute-start.9 = (f32[640,256]{1,0:T(8,128)}, f32[640,256]{1,0:T(8,128)S(1)}, u32[]{:S(2)}, u32[]{:S(2)}) collective-permute-start(f32[640,256]{1,0:T(8,128)} %get-tuple-element.20.refs_9_), channel_id=1, source_target_pairs={{0,28},{4,8},{8,4},{12,16},{16,12},{20,24},{24,20},{28,0},{1,29},{... | collective-permute-start | bytes 1966088 | tf_op jit(solution)/shard_map/ppermute | solution.py:356
  24.0 1.5 %collective-permute-start.1 = (f32[2,64,512]{2,1,0:T(8,128)S(1)}, f32[2,64,512]{2,1,0:T(8,128)S(1)}, u32[]{:S(2)}, u32[]{:S(2)}) collective-permute-start(f32[2,64,512]{2,1,0:T(8,128)S(1)} %bitcast.14), channel_id=1, source_target_pairs={{0,2},{1,3},{2,0},{3,1},{4,6},{5,7},{6,4},{7,5},{8,10},{9,11},{10,... | collective-permute-start | bytes 786440 | tf_op jit(solution)/shard_map/ppermute | solution.py:312
  26.1 4.3 %collective-permute-done.1.refs_2_ = f32[2,64,512]{2,1,0:T(8,128)S(1)} collective-permute-done((f32[2,64,512]{2,1,0:T(8,128)S(1)}, f32[2,64,512]{2,1,0:T(8,128)S(1)}, u32[]{:S(2)}, u32[]{:S(2)}) %collective-permute-start.1) | collective-permute-done | bytes 262176 | tf_op jit(solution)/shard_map/ppermute | solution.py:312
  30.4 1.2 %collective-permute-start.2 = (f32[1,64,512]{2,1,0:T(8,128)S(1)}, f32[1,64,512]{2,1,0:T(8,128)S(1)}, u32[]{:S(2)}, u32[]{:S(2)}) collective-permute-start(f32[1,64,512]{2,1,0:T(8,128)S(1)} %slice.24), channel_id=1, source_target_pairs={{0,1},{1,0},{2,3},{3,2},{4,5},{5,4},{6,7},{7,6},{8,9},{9,8},{10,11... | collective-permute-start | bytes 393224 | tf_op jit(solution)/shard_map/ppermute | solution.py:313
  31.6 1.7 %collective-permute-done.refs_1_ = f32[2,64,512]{2,1,0:T(8,128)S(1)} collective-permute-done((f32[2,64,512]{2,1,0:T(8,128)S(1)}, f32[2,64,512]{2,1,0:T(8,128)S(1)}, u32[]{:S(2)}, u32[]{:S(2)}) %collective-permute-start) | collective-permute-done | bytes 262176 | tf_op jit(solution)/shard_map/ppermute | solution.py:311
  33.4 2.0 %collective-permute-done.2.refs_3_ = f32[1,64,512]{2,1,0:T(8,128)S(1)} collective-permute-done((f32[1,64,512]{2,1,0:T(8,128)S(1)}, f32[1,64,512]{2,1,0:T(8,128)S(1)}, u32[]{:S(2)}, u32[]{:S(2)}) %collective-permute-start.2) | collective-permute-done | bytes 131104 | tf_op jit(solution)/shard_map/ppermute | solution.py:313
  35.4 2.9 %collective-permute-done.3.refs_4_ = f32[1,64,512]{2,1,0:T(8,128)S(1)} collective-permute-done((f32[1,64,512]{2,1,0:T(8,128)S(1)}, f32[1,64,512]{2,1,0:T(8,128)S(1)}, u32[]{:S(2)}, u32[]{:S(2)}) %collective-permute-start.3) | collective-permute-done | bytes 131104 | tf_op jit(solution)/shard_map/ppermute | solution.py:314
  39.6 19.0 %shard_map.38 = (f32[2,256,512]{2,1,0:T(8,128)}, f32[1024,256]{1,0:T(8,128)}, f32[384,256]{1,0:T(8,128)}, f32[384,512]{1,0:T(8,128)}, f32[640,768]{1,0:T(8,128)}...) custom-call(s32[9]{0:T(128)} %stack.44.index_ref, f32[2,64,512]{2,1,0:T(8,128)} %bitcast.13, f32[2,64,512]{2,1,0:T(8,128)} %copy-done.9, ...), custom_call_target="tpu_custom_call" | custom-call | flops 14092861440 | bytes 11534372 | tf_op jit(solution)/shard_map/pallas_call | solution.py:295
  58.6 2.9 %collective-permute-done.10.got_ref = f32[1024,256]{1,0:T(8,128)S(1)} collective-permute-done((f32[1024,256]{1,0:T(8,128)}, f32[1024,256]{1,0:T(8,128)S(1)}, u32[]{:S(2)}, u32[]{:S(2)}) %collective-permute-start.10) | collective-permute-done | bytes 1048608 | tf_op jit(solution)/shard_map/ppermute | solution.py:367
  61.5 1.0 copy-done.10
  62.5 3.3 %shard_map.39 = (f32[768,256]{1,0:T(8,128)}, f32[64,512]{1,0:T(8,128)}) custom-call(s32[9]{0:T(128)} %stack.44.index_ref, f32[1024,256]{1,0:T(8,128)} %get-tuple-element.21.own_ref, f32[1024,256]{1,0:T(8,128)} %copy-done.10), custom_call_target="tpu_custom_call" | custom-call | flops 603979776 | bytes 3014692 | tf_op jit(solution)/shard_map/pallas_call | solution.py:295
  65.8 1.4 %collective-permute-start.11 = (f32[64,512]{1,0:T(8,128)}, f32[64,512]{1,0:T(8,128)S(1)}, u32[]{:S(2)}, u32[]{:S(2)}) collective-permute-start(f32[64,512]{1,0:T(8,128)} %get-tuple-element.22.start_ref), channel_id=1, source_target_pairs={{8,0},{12,4},{16,8},{20,12},{24,16},{28,20},{9,1},{13,5},{17,9},{2... | collective-permute-start | bytes 393224 | tf_op jit(solution)/shard_map/ppermute | solution.py:377
  67.2 2.1 %collective-permute-start.15 = (f32[384,256]{1,0:T(8,128)S(1)}, f32[384,256]{1,0:T(8,128)S(1)}, u32[]{:S(2)}, u32[]{:S(2)}) collective-permute-start(f32[384,256]{1,0:T(8,128)S(1)} %copy-done.13), channel_id=1, source_target_pairs={{0,4},{4,8},{8,12},{12,16},{16,20},{20,24},{24,28},{1,5},{5,9},{9,... | collective-permute-start | bytes 1179656 | tf_op jit(solution)/shard_map/ppermute | solution.py:368
  69.3 4.3 %collective-permute-done.11.got_ref = f32[64,512]{1,0:T(8,128)S(1)} collective-permute-done((f32[64,512]{1,0:T(8,128)}, f32[64,512]{1,0:T(8,128)S(1)}, u32[]{:S(2)}, u32[]{:S(2)}) %collective-permute-start.11) | collective-permute-done | bytes 131104 | tf_op jit(solution)/shard_map/ppermute | solution.py:377
  74.2 2.2 %shard_map.40 = f32[64,512]{1,0:T(8,128)} custom-call(f32[64,512]{1,0:T(8,128)} %get-tuple-element.22.start_ref, f32[768,256]{1,0:T(8,128)} %get-tuple-element.23.chain_ref, f32[64,512]{1,0:T(8,128)} %copy-done.2), custom_call_target="tpu_custom_call" | custom-call | flops 100663296 | bytes 1179648 | tf_op jit(solution)/shard_map/pallas_call | solution.py:295
  76.4 1.3 %collective-permute-start.12 = (f32[64,512]{1,0:T(8,128)}, f32[64,512]{1,0:T(8,128)S(1)}, u32[]{:S(2)}, u32[]{:S(2)}) collective-permute-start(f32[64,512]{1,0:T(8,128)} %shard_map.40), channel_id=1, source_target_pairs={{8,0},{12,4},{16,8},{20,12},{24,16},{28,20},{9,1},{13,5},{17,9},{2... | collective-permute-start | bytes 393224 | tf_op jit(solution)/shard_map/ppermute | solution.py:377
  77.6 5.8 %collective-permute-done.12.got_ref = f32[64,512]{1,0:T(8,128)S(1)} collective-permute-done((f32[64,512]{1,0:T(8,128)}, f32[64,512]{1,0:T(8,128)S(1)}, u32[]{:S(2)}, u32[]{:S(2)}) %collective-permute-start.12) | collective-permute-done | bytes 131104 | tf_op jit(solution)/shard_map/ppermute | solution.py:377
  84.0 2.2 %shard_map.41 = f32[64,512]{1,0:T(8,128)} custom-call(f32[64,512]{1,0:T(8,128)} %get-tuple-element.22.start_ref, f32[768,256]{1,0:T(8,128)} %get-tuple-element.23.chain_ref, f32[64,512]{1,0:T(8,128)} %copy-done.3), custom_call_target="tpu_custom_call" | custom-call | flops 100663296 | bytes 1179648 | tf_op jit(solution)/shard_map/pallas_call | solution.py:295
  86.2 1.3 %collective-permute-start.13 = (f32[64,512]{1,0:T(8,128)}, f32[64,512]{1,0:T(8,128)S(1)}, u32[]{:S(2)}, u32[]{:S(2)}) collective-permute-start(f32[64,512]{1,0:T(8,128)} %shard_map.41), channel_id=1, source_target_pairs={{8,0},{12,4},{16,8},{20,12},{24,16},{28,20},{9,1},{13,5},{17,9},{2... | collective-permute-start | bytes 393224 | tf_op jit(solution)/shard_map/ppermute | solution.py:377
  87.5 0.8 slice.22.straddle_ref
  88.4 0.9 slice.23.wide_ref
  89.2 4.1 %collective-permute-done.13.own_ref = f32[64,512]{1,0:T(8,128)S(1)} collective-permute-done((f32[64,512]{1,0:T(8,128)}, f32[64,512]{1,0:T(8,128)S(1)}, u32[]{:S(2)}, u32[]{:S(2)}) %collective-permute-start.13) | collective-permute-done | bytes 131104 | tf_op jit(solution)/shard_map/ppermute | solution.py:377
  94.1 6.8 %shard_map.42 = (f32[128,512]{1,0:T(8,128)}, f32[512,512]{1,0:T(8,128)}) custom-call(s32[9]{0:T(128)} %stack.44.index_ref, f32[1024,256]{1,0:T(8,128)} %get-tuple-element.21.own_ref, f32[1024,256]{1,0:T(8,128)} %copy-done.10, f32[384,256]{1,0:T(8,128)} %copy-done.14, f32[384,512]{1,0:T(8,128)} %get-tuple-element.25.now_ref, ...), custom_call_target="tpu_custom_call" | custom-call | flops 3019898880 | bytes 7864356 | tf_op jit(solution)/shard_map/pallas_call | solution.py:295
  101.5 2.7 %shard_map.43 = f32[512,128]{1,0:T(8,128)} custom-call(s32[9]{0:T(128)} %stack.44.index_ref, f32[64,512]{1,0:T(8,128)} %copy-done.4, f32[64,512]{1,0:T(8,128)} %copy-done.5, f32[128,512]{1,0:T(8,128)} %get-tuple-element.29.base_ref, f32[512,512]{1,0:T(8,128)} %get-tuple-element.30.reply_ref), custom_call_target="tpu_custom_call" | custom-call | flops 402653184 | bytes 1835044 | tf_op jit(solution)/shard_map/pallas_call | solution.py:295
  (54 shorter events, 6.0 us)
Async XLA Ops:
  0.0 24.0 %copy-start.15 = (f32[2,512,64]{1,2,0:T(8,128)S(1)}, f32[2,512,64]{1,2,0:T(8,128)}, u32[]{:S(2)}) copy-start(f32[2,512,64]{1,2,0:T(8,128)} %param.4) | copy-start | bytes 786436
  0.0 9.5 %collective-permute-start.5 = (f32[2,64,512]{2,1,0:T(8,128)}, f32[2,64,512]{2,1,0:T(8,128)S(1)}, u32[]{:S(2)}, u32[]{:S(2)}) collective-permute-start(f32[2,64,512]{2,1,0:T(8,128)} %bitcast.10), channel_id=1, source_target_pairs={{0,2},{1,3},{2,0},{3,1},{4,6},{5,7},{6,4},{7,5},{8,10},{9,11},{10,... | collective-permute-start | bytes 786440 | tf_op jit(solution)/shard_map/ppermute | solution.py:312
  3.0 8.3 %collective-permute-start.4 = (f32[2,64,512]{2,1,0:T(8,128)}, f32[2,64,512]{2,1,0:T(8,128)S(1)}, u32[]{:S(2)}, u32[]{:S(2)}) collective-permute-start(f32[2,64,512]{2,1,0:T(8,128)} %bitcast.11), channel_id=1, source_target_pairs={{0,1},{1,0},{2,3},{3,2},{4,5},{5,4},{6,7},{7,6},{8,9},{9,8},{10,11... | collective-permute-start | bytes 786440 | tf_op jit(solution)/shard_map/ppermute | solution.py:311
  9.5 6.9 %copy-start.6 = (f32[2,64,512]{2,1,0:T(8,128)}, f32[2,64,512]{2,1,0:T(8,128)S(1)}, u32[]{:S(2)}) copy-start(f32[2,64,512]{2,1,0:T(8,128)S(1)} %collective-permute-done.5.refs_2_) | copy-start | bytes 786436
  9.5 5.0 %collective-permute-start.6 = (f32[1,64,512]{2,1,0:T(8,128)S(1)}, f32[1,64,512]{2,1,0:T(8,128)S(1)}, u32[]{:S(2)}, u32[]{:S(2)}) collective-permute-start(f32[1,64,512]{2,1,0:T(8,128)S(1)} %slice.26), channel_id=1, source_target_pairs={{0,1},{1,0},{2,3},{3,2},{4,5},{5,4},{6,7},{7,6},{8,9},{9,8},{10,11... | collective-permute-start | bytes 393224 | tf_op jit(solution)/shard_map/ppermute | solution.py:313
  11.3 5.1 %copy-start.7 = (f32[2,64,512]{2,1,0:T(8,128)}, f32[2,64,512]{2,1,0:T(8,128)S(1)}, u32[]{:S(2)}) copy-start(f32[2,64,512]{2,1,0:T(8,128)S(1)} %collective-permute-done.4.refs_1_) | copy-start | bytes 786436
  11.3 5.0 %collective-permute-start.7 = (f32[1,64,512]{2,1,0:T(8,128)S(1)}, f32[1,64,512]{2,1,0:T(8,128)S(1)}, u32[]{:S(2)}, u32[]{:S(2)}) collective-permute-start(f32[1,64,512]{2,1,0:T(8,128)S(1)} %slice.27), channel_id=1, source_target_pairs={{0,2},{1,3},{2,0},{3,1},{4,6},{5,7},{6,4},{7,5},{8,10},{9,11},{10,... | collective-permute-start | bytes 393224 | tf_op jit(solution)/shard_map/ppermute | solution.py:314
  14.6 1.8 %copy-start.16 = (f32[1,64,512]{2,1,0:T(8,128)}, f32[1,64,512]{2,1,0:T(8,128)S(1)}, u32[]{:S(2)}) copy-start(f32[1,64,512]{2,1,0:T(8,128)S(1)} %collective-permute-done.6.refs_3_) | copy-start | bytes 393220
  20.3 18.1 %collective-permute-start.8 = (f32[640,256]{1,0:T(8,128)}, f32[640,256]{1,0:T(8,128)S(1)}, u32[]{:S(2)}, u32[]{:S(2)}) collective-permute-start(f32[640,256]{1,0:T(8,128)} %get-tuple-element.19.refs_7_), channel_id=1, source_target_pairs={{0,4},{4,0},{8,12},{12,8},{16,20},{20,16},{24,28},{28,24},{1,5},{5... | collective-permute-start | bytes 1966088 | tf_op jit(solution)/shard_map/ppermute | solution.py:355
  20.3 18.5 %collective-permute-start.9 = (f32[640,256]{1,0:T(8,128)}, f32[640,256]{1,0:T(8,128)S(1)}, u32[]{:S(2)}, u32[]{:S(2)}) collective-permute-start(f32[640,256]{1,0:T(8,128)} %get-tuple-element.20.refs_9_), channel_id=1, source_target_pairs={{0,28},{4,8},{8,4},{12,16},{16,12},{20,24},{24,20},{28,0},{1,29},{... | collective-permute-start | bytes 1966088 | tf_op jit(solution)/shard_map/ppermute | solution.py:356
  24.0 6.4 %collective-permute-start.1 = (f32[2,64,512]{2,1,0:T(8,128)S(1)}, f32[2,64,512]{2,1,0:T(8,128)S(1)}, u32[]{:S(2)}, u32[]{:S(2)}) collective-permute-start(f32[2,64,512]{2,1,0:T(8,128)S(1)} %bitcast.14), channel_id=1, source_target_pairs={{0,2},{1,3},{2,0},{3,1},{4,6},{5,7},{6,4},{7,5},{8,10},{9,11},{10,... | collective-permute-start | bytes 786440 | tf_op jit(solution)/shard_map/ppermute | solution.py:312
  25.5 7.8 %collective-permute-start = (f32[2,64,512]{2,1,0:T(8,128)S(1)}, f32[2,64,512]{2,1,0:T(8,128)S(1)}, u32[]{:S(2)}, u32[]{:S(2)}) collective-permute-start(f32[2,64,512]{2,1,0:T(8,128)S(1)} %bitcast.15), channel_id=1, source_target_pairs={{0,1},{1,0},{2,3},{3,2},{4,5},{5,4},{6,7},{7,6},{8,9},{9,8},{10,11... | collective-permute-start | bytes 786440 | tf_op jit(solution)/shard_map/ppermute | solution.py:311
  30.4 8.4 %copy-start.8 = (f32[2,64,512]{2,1,0:T(8,128)}, f32[2,64,512]{2,1,0:T(8,128)S(1)}, u32[]{:S(2)}) copy-start(f32[2,64,512]{2,1,0:T(8,128)S(1)} %collective-permute-done.1.refs_2_) | copy-start | bytes 786436
  30.4 5.0 %collective-permute-start.2 = (f32[1,64,512]{2,1,0:T(8,128)S(1)}, f32[1,64,512]{2,1,0:T(8,128)S(1)}, u32[]{:S(2)}, u32[]{:S(2)}) collective-permute-start(f32[1,64,512]{2,1,0:T(8,128)S(1)} %slice.24), channel_id=1, source_target_pairs={{0,1},{1,0},{2,3},{3,2},{4,5},{5,4},{6,7},{7,6},{8,9},{9,8},{10,11... | collective-permute-start | bytes 393224 | tf_op jit(solution)/shard_map/ppermute | solution.py:313
  33.3 5.5 %copy-start.9 = (f32[2,64,512]{2,1,0:T(8,128)}, f32[2,64,512]{2,1,0:T(8,128)S(1)}, u32[]{:S(2)}) copy-start(f32[2,64,512]{2,1,0:T(8,128)S(1)} %collective-permute-done.refs_1_) | copy-start | bytes 786436
  33.3 5.0 %collective-permute-start.3 = (f32[1,64,512]{2,1,0:T(8,128)S(1)}, f32[1,64,512]{2,1,0:T(8,128)S(1)}, u32[]{:S(2)}, u32[]{:S(2)}) collective-permute-start(f32[1,64,512]{2,1,0:T(8,128)S(1)} %slice.25), channel_id=1, source_target_pairs={{0,2},{1,3},{2,0},{3,1},{4,6},{5,7},{6,4},{7,5},{8,10},{9,11},{10,... | collective-permute-start | bytes 393224 | tf_op jit(solution)/shard_map/ppermute | solution.py:314
  35.4 3.3 %copy-start.18 = (f32[1,64,512]{2,1,0:T(8,128)}, f32[1,64,512]{2,1,0:T(8,128)S(1)}, u32[]{:S(2)}) copy-start(f32[1,64,512]{2,1,0:T(8,128)S(1)} %collective-permute-done.2.refs_3_) | copy-start | bytes 393220
  38.3 0.9 copy-start.11
  38.7 0.8 copy-start.12
  58.5 8.7 %copy-start.13 = (f32[384,256]{1,0:T(8,128)S(1)}, f32[384,256]{1,0:T(8,128)}, u32[]{:S(2)}) copy-start(f32[384,256]{1,0:T(8,128)} %get-tuple-element.24) | copy-start | bytes 1179652
  58.5 29.0 %copy-start = (f32[2,256,512]{2,1,0:T(8,128)S(1)}, f32[2,256,512]{2,1,0:T(8,128)}, u32[]{:S(2)}) copy-start(f32[2,256,512]{2,1,0:T(8,128)} %get-tuple-element.18.refs_6_) | copy-start | bytes 3145732
  58.6 2.9 %collective-permute-start.10 = (f32[1024,256]{1,0:T(8,128)}, f32[1024,256]{1,0:T(8,128)S(1)}, u32[]{:S(2)}, u32[]{:S(2)}) collective-permute-start(f32[1024,256]{1,0:T(8,128)} %get-tuple-element.21.own_ref), channel_id=1, source_target_pairs={{0,4},{4,0},{8,12},{12,8},{16,20},{20,16},{24,28},{28,24},{1,5},{5... | collective-permute-start | bytes 3145736 | tf_op jit(solution)/shard_map/ppermute | solution.py:367
  61.5 1.0 copy-start.10
  65.8 22.6 %copy-start.1 = (f32[2,256,512]{2,1,0:T(8,128)S(1)}, f32[2,256,512]{2,1,0:T(8,128)}, u32[]{:S(2)}) copy-start(f32[2,256,512]{2,1,0:T(8,128)} %get-tuple-element.28) | copy-start | bytes 3145732
  65.8 7.8 %collective-permute-start.11 = (f32[64,512]{1,0:T(8,128)}, f32[64,512]{1,0:T(8,128)S(1)}, u32[]{:S(2)}, u32[]{:S(2)}) collective-permute-start(f32[64,512]{1,0:T(8,128)} %get-tuple-element.22.start_ref), channel_id=1, source_target_pairs={{8,0},{12,4},{16,8},{20,12},{24,16},{28,20},{9,1},{13,5},{17,9},{2... | collective-permute-start | bytes 393224 | tf_op jit(solution)/shard_map/ppermute | solution.py:377
  67.2 26.1 %collective-permute-start.15 = (f32[384,256]{1,0:T(8,128)S(1)}, f32[384,256]{1,0:T(8,128)S(1)}, u32[]{:S(2)}, u32[]{:S(2)}) collective-permute-start(f32[384,256]{1,0:T(8,128)S(1)} %copy-done.13), channel_id=1, source_target_pairs={{0,4},{4,8},{8,12},{12,16},{16,20},{20,24},{24,28},{1,5},{5,9},{9,... | collective-permute-start | bytes 1179656 | tf_op jit(solution)/shard_map/ppermute | solution.py:368
  73.5 0.7 copy-start.2
  76.4 7.1 %collective-permute-start.12 = (f32[64,512]{1,0:T(8,128)}, f32[64,512]{1,0:T(8,128)S(1)}, u32[]{:S(2)}, u32[]{:S(2)}) collective-permute-start(f32[64,512]{1,0:T(8,128)} %shard_map.40), channel_id=1, source_target_pairs={{8,0},{12,4},{16,8},{20,12},{24,16},{28,20},{9,1},{13,5},{17,9},{2... | collective-permute-start | bytes 393224 | tf_op jit(solution)/shard_map/ppermute | solution.py:377
  86.2 7.1 %collective-permute-start.13 = (f32[64,512]{1,0:T(8,128)}, f32[64,512]{1,0:T(8,128)S(1)}, u32[]{:S(2)}, u32[]{:S(2)}) collective-permute-start(f32[64,512]{1,0:T(8,128)} %shard_map.41), channel_id=1, source_target_pairs={{8,0},{12,4},{16,8},{20,12},{24,16},{28,20},{9,1},{13,5},{17,9},{2... | collective-permute-start | bytes 393224 | tf_op jit(solution)/shard_map/ppermute | solution.py:377
  93.3 7.6 %copy-start.4 = (f32[64,512]{1,0:T(8,128)}, f32[64,512]{1,0:T(8,128)S(1)}, u32[]{:S(2)}) copy-start(f32[64,512]{1,0:T(8,128)S(1)} %collective-permute-done.13.own_ref) | copy-start | bytes 393220
  93.3 7.6 %collective-permute-start.14 = (f32[64,512]{1,0:T(8,128)S(1)}, f32[64,512]{1,0:T(8,128)S(1)}, u32[]{:S(2)}, u32[]{:S(2)}) collective-permute-start(f32[64,512]{1,0:T(8,128)S(1)} %collective-permute-done.13.own_ref), channel_id=1, source_target_pairs={{0,4},{4,0},{8,12},{12,8},{16,20},{20,16},{24,28},{28,24},{1,5},{5... | collective-permute-start | bytes 393224 | tf_op jit(solution)/shard_map/ppermute | solution.py:390
  93.3 0.8 copy-start.14
  (4 other events, 2.6 us)
where the time goes:
time: 105 us; the launch traced here: 104 us
  Pallas kernels  39.3 us (37%)
  waiting for transfers between devices  36.1 us (34%)
  starting transfers between devices  21.1 us (20%)
  local copies, waits for them, and re-layouts  7.59 us (7%)
    pallas_call x7, Pallas kernels, call(): pl.pallas_call(body, out_shape=shapes, in_specs=first + [space] * (len(op...  39.3 us
    ppermute x3, waiting for transfers between devices, on_device(): got = lax.ppermute(carry, 'row', down)  14.1 us
    ppermute x2, waiting for transfers between devices, gathered(): side = lax.ppermute(shard, axis, swaps[1])  9.3 us
    unnamed x40, local copies, waits for them, and re-layouts  5.19 us
    ppermute x2, waiting for transfers between devices, gathered(): far_second = lax.ppermute(near[1:2], axis, swaps[1])  4.72 us
    ppermute x2, starting transfers between devices, gathered(): side = lax.ppermute(shard, axis, swaps[1])  4.51 us
    ppermute x3, starting transfers between devices, on_device(): got = lax.ppermute(carry, 'row', down)  3.97 us
    ppermute x1, starting transfers between devices, on_device(): outer_got = lax.ppermute(outer, 'row', outside_route)  3.71 us
  transfers between devices with their start and end apart: 16, of which 12 were waited for; matrix products, arithmetic and copies ran while one was open for 2% of the time, Pallas kernels for 11%

commit v1 on v0

v1 whole, which is shorter than its diff:
```python
import functools

import jax
import jax.numpy as jnp
from jax import lax
from jax.experimental import pallas as pl
from jax.experimental.pallas import tpu as pltpu
from jax.sharding import PartitionSpec as P


F32 = jnp.float32
BF16 = jnp.bfloat16
BASE_BLOCK = 32
LANES = 128
PAD = 8
VMEM_GRANT = 16 * 1024 * 1024


def split(value):
    high = value.astype(BF16)
    return high, (value - high.astype(F32)).astype(BF16)


def raw_dot(left, right, transposed):
    dims = (((1,), (1 if transposed else 0,)), ((), ()))
    return lax.dot_general(left, right, dims, preferred_element_type=F32)


def product(left, right, transposed=False):
    left = left if isinstance(left, tuple) else split(left)
    right = right if isinstance(right, tuple) else split(right)
    return (
        raw_dot(left[0], right[0], transposed)
        + raw_dot(left[0], right[1], transposed)
        + raw_dot(left[1], right[0], transposed)
    )


def cut(pair, rows=slice(None), lanes=slice(None)):
    return pair[0][rows, lanes], pair[1][rows, lanes]


def stack(*values):
    return jnp.concatenate(values, axis=0)


def beside(*values):
    return jnp.concatenate(values, axis=1)


def block_inverse(packed, base):
    done = []
    for start in range(0, packed.shape[1], LANES):
        entries = packed[:, start : start + LANES]
        rows = lax.broadcasted_iota(jnp.int32, entries.shape, 0)
        lanes = lax.broadcasted_iota(jnp.int32, entries.shape, 1)
        group = (lanes // base) * base
        value = jnp.where(rows == lanes - group, 1.0, 0.0).astype(F32)
        for step in range(base - 1):
            top = (step // 8) * 8
            factor = jnp.take_along_axis(entries[top:], (group + step)[top:], axis=1)
            changed = value[top:] - factor * value[step : step + 1]
            value = stack(value[:top], changed) if top else changed
        done.append(value)
    return beside(*done)


def small_inverse(strict, across, base):
    order = strict.shape[0]
    lanes = lax.broadcasted_iota(jnp.int32, (base, order), 1) // base
    packed = jnp.zeros((base, order), F32)
    for block in range(order // base):
        packed = jnp.where(lanes == block, strict[block * base : (block + 1) * base], packed)
    solved = block_inverse(packed * across, base)
    return stack(*[jnp.where(lanes == block, solved, 0.0) for block in range(order // base)])


def lower_inverses(stricts, diagonals):
    order = stricts[0].shape[0]
    base = min(BASE_BLOCK, order)
    rows = lax.broadcasted_iota(jnp.int32, (order, order), 0)
    lanes = lax.broadcasted_iota(jnp.int32, (order, order), 1)
    result = []
    for strict, diagonal in zip(stricts, diagonals):
        across = 2.0 / diagonal
        along = jnp.sum(jnp.where(rows == lanes, across, 0.0), axis=1, keepdims=True)
        result.append(small_inverse(strict, across, base) * along)
    size = base
    while 2 * size < order:
        here = (rows // (2 * size) == lanes // (2 * size)) & (rows // size != lanes // size)
        wholes = [split(now) for now in result]
        starts = range(0, order, 2 * size)
        odds = [
            tuple(stack(*[part[at + size : at + 2 * size] for at in starts]) for part in whole)
            for whole in wholes
        ]
        inner = [
            product(odd, jnp.where(here, strict, 0.0)) for odd, strict in zip(odds, stricts)
        ]
        outer = [product(value, whole) for value, whole in zip(inner, wholes)]
        merged = []
        for now, change in zip(result, outer):
            bands = []
            for number, at in enumerate(starts):
                bands.append(now[at : at + size])
                bands.append(
                    now[at + size : at + 2 * size] - change[number * size : (number + 1) * size]
                )
            merged.append(stack(*bands))
        result = merged
        size *= 2
    if size < order:
        wholes = [split(now) for now in result]
        low, high = slice(0, size), slice(size, None)
        inner = [
            product(cut(whole, high, high), strict[high, low])
            for whole, strict in zip(wholes, stricts)
        ]
        outer = [product(value, cut(whole, low, low)) for value, whole in zip(inner, wholes)]
        result = [
            stack(now[low], beside(-change, now[high, high]))
            for now, change in zip(result, outer)
        ]
    return result


def place(pieces, index_ref, first, target, width):
    for at, (piece, sweeps) in enumerate(pieces):
        start = pl.multiple_of(index_ref[first + at] * width, width)
        for sweep, source in sweeps:
            target[sweep, pl.ds(start, width), :] = piece[source]


def triangle(order):
    rows = lax.broadcasted_iota(jnp.int32, (order, order), 0)
    lanes = lax.broadcasted_iota(jnp.int32, (order, order), 1)
    return rows > lanes, rows == lanes


def pack_grams(target, pair, below, diagonal):
    half = pair[0].shape[0]
    target[0:half, :] = jnp.where(below, pair[0], pair[1])
    for at, gram in enumerate(pair):
        target[half + at : half + at + 1, :] = jnp.sum(
            jnp.where(diagonal, gram, 0.0), axis=0, keepdims=True
        )


def gram_kernel(layout, width, half, index_ref, *refs):
    count = len(layout)
    pieces = [(refs[at], layout[at]) for at in range(count)]
    matrix_ref, wide_ref, inner_ref, outer_ref = refs[count:]
    place(pieces, index_ref, 4, wide_ref, width)
    even = index_ref[0] == 0
    below, diagonal = triangle(half)
    lows, highs = [], []
    for sweep in range(2):
        whole = split(wide_ref[sweep])
        low, high = cut(whole, lanes=slice(0, half)), cut(whole, lanes=slice(half, None))
        lows.append(product(low, low, True))
        highs.append(product(high, high, True))
        if sweep == 0:
            first = product(jnp.transpose(matrix_ref[half:, :]), high, True)
    top = slice(half + PAD, None)
    inner_ref[top, :] = first
    outer_ref[top, :] = first
    pack_grams(inner_ref, [jnp.where(even, b, a) for a, b in zip(lows, highs)], below, diagonal)
    pack_grams(outer_ref, [jnp.where(even, a, b) for a, b in zip(lows, highs)], below, diagonal)


def local_kernel(layout, width, half, index_ref, *refs):
    count = len(layout)
    pieces = [(refs[at], layout[at]) for at in range(count)]
    (
        matrix_ref, straddle_ref, inner_ref, inner_got_ref, outer_ref, outer_got_ref,
        wide_ref, step_ref, up_ref, state_ref, seen_ref, square_ref, factor_ref,
    ) = refs[count:]
    place(pieces, index_ref, 4, wide_ref, width)
    parity = index_ref[0]
    even = parity == 0
    outside = jnp.where(index_ref[1] == 0, 1.0, 0.0)
    columns = matrix_ref.shape[1]
    below, diagonal = triangle(half)
    blank = jnp.zeros((half, half), F32)
    low_lanes, high_lanes = slice(0, half), slice(half, None)

    current = jnp.transpose(matrix_ref[...])
    whole = split(current)
    upper, lower = cut(whole, lanes=low_lanes), cut(whole, lanes=high_lanes)
    straddle = [split(straddle_ref[sweep]) for sweep in range(2)]
    aligned = [split(wide_ref[sweep]) for sweep in range(2)]
    bottom = [cut(value, lanes=low_lanes) for value in straddle]
    top = [cut(value, lanes=high_lanes) for value in straddle]
    first = [cut(value, lanes=low_lanes) for value in aligned]
    last = [cut(value, lanes=high_lanes) for value in aligned]

    inner = inner_ref[0 : half + PAD, :] + inner_got_ref[0 : half + PAD, :]
    outer = outer_ref[0 : half + PAD, :] + outside * outer_got_ref[0 : half + PAD, :]
    stricts, diagonals = [], []
    for packed in (inner, outer):
        mixed = packed[0:half]
        stricts.append(jnp.where(below, mixed, 0.0))
        stricts.append(jnp.where(below, jnp.transpose(mixed), 0.0))
        diagonals.append(packed[half : half + 1])
        diagonals.append(packed[half + 1 : half + 2])
    for value in aligned:
        gram = product(value, value, True)
        stricts.append(jnp.where(below, gram, 0.0))
        diagonals.append(jnp.sum(jnp.where(diagonal, gram, 0.0), axis=0, keepdims=True))
    factors = lower_inverses(stricts, diagonals)

    through = [product(t, a, True) for t, a in zip(top, last)]
    onward = [product(a, b, True) for a, b in zip(first, bottom)]
    seen0, seen1 = (product(whole, value, True) for value in aligned)
    raw0, raw1 = (product(upper, value, True) for value in bottom)
    second = product(lower, top[1], True)
    cross_aligned = split(product(aligned[0], aligned[1], True))
    cross_bottom_aligned = split(product(bottom[0], first[1], True))
    cross_top_aligned = split(product(top[0], last[1], True))
    cross_top = split(product(top[0], top[1], True))
    cross_aligned_top = split(product(last[0], top[1], True))
    cross_aligned_bottom = split(product(first[0], bottom[1], True))
    cross_bottom = split(product(bottom[0], bottom[1], True))

    for sweep in range(2):
        square_ref[sweep, parity] = factors[sweep]
        square_ref[sweep, 1 - parity] = factors[2 + sweep]
    factor_top = [split(square_ref[sweep, 0]) for sweep in range(2)]
    factor_bottom = split(square_ref[0, 1])
    factor_aligned = [split(value) for value in factors[4:]]
    rows = slice(half + PAD, None)
    own_first = inner_ref[rows, :]
    got_first = jnp.where(even, outside * outer_got_ref[rows, :], inner_got_ref[rows, :])

    reached = [product(f, value) for f, value in zip(factor_top, through)]
    leaving = [product(f, value) for f, value in zip(factor_aligned, onward)]
    reached_pair = [split(value) for value in reached]
    leaving_pair = [split(value) for value in leaving]
    own_pair = split(own_first)
    step1 = product(reached_pair[1], leaving_pair[1])
    outer_coeff = stack(product(own_pair, factor_top[0]), square_ref[0, 0])
    inside = split(stack(seen0 - product(own_pair, reached_pair[0]), -reached[0]))
    carry0 = stack(raw0, blank) - product(inside, leaving_pair[0])
    coeffs = product(inside, factor_aligned[0])
    back = product(stack(carry0[:columns] + got_first, carry0[columns:]), factor_bottom)
    outer_pair, coeff_pair, back_pair = split(outer_coeff), split(coeffs), split(back)
    begun = (
        stack(second, blank)
        - product(outer_pair, cross_top)
        - product(coeff_pair, cross_aligned_top)
    )
    seen = (
        stack(seen1, blank)
        - product(coeff_pair, cross_aligned)
        - product(outer_pair, cross_top_aligned)
        - product(back_pair, cross_bottom_aligned)
    )
    raw = (
        stack(raw1, blank)
        - product(coeff_pair, cross_aligned_bottom)
        - product(back_pair, cross_bottom)
    )
    carry1 = raw - product(seen, leaving_pair[1]) + product(begun, step1)
    up_ref[...] = begun
    seen_ref[...] = seen
    state_ref[:, 0:half] = outer_coeff
    state_ref[:, half : 2 * half] = coeffs
    state_ref[:, 2 * half :] = back
    factor_ref[0] = square_ref[1, 0]
    factor_ref[1] = square_ref[1, 1]
    factor_ref[2] = factors[5]
    factor_ref[3] = reached[1]
    step_ref[0:half, :] = carry0[columns:]
    step_ref[half : 2 * half, :] = carry1[columns:]
    step_ref[2 * half : 3 * half, :] = step1
    step_ref[3 * half : 3 * half + columns, :] = carry0[:columns]
    step_ref[3 * half + columns :, :] = carry1[:columns]


def by_core(index_ref, body, own_ref, got_ref):
    @pl.when(index_ref[0] == 0)
    def _():
        body(own_ref, got_ref)

    @pl.when(index_ref[0] != 0)
    def _():
        body(got_ref, own_ref)


def compose_kernel(half, index_ref, own_ref, got_ref, high_ref, low_ref, start_ref):
    part = start_ref.shape[0]

    def store(at, value):
        high, low = split(value)
        high_ref[at * half : (at + 1) * half, :] = high
        low_ref[at * half : (at + 1) * half, :] = low

    def body(even_ref, odd_ref):
        even0, even_mix, even1 = (
            split(even_ref[at * half : (at + 1) * half, :]) for at in range(3)
        )
        odd0, odd_mix, odd1 = (split(odd_ref[at * half : (at + 1) * half, :]) for at in range(3))

        def rows(ref, sweep):
            first = pl.multiple_of(3 * half + 2 * sweep * part + index_ref[0] * part, 8)
            return ref[pl.ds(first, part), :]

        odd_first = split(rows(odd_ref, 0))
        start_ref[:, :half] = rows(even_ref, 0) + product(odd_first, even0)
        start_ref[:, half:] = (
            rows(even_ref, 1) + product(odd_first, even_mix) + product(rows(odd_ref, 1), even1)
        )
        store(0, product(odd0, even0))
        store(1, product(odd0, even_mix) + product(odd_mix, even1))
        store(2, product(odd1, even1))

    by_core(index_ref, body, own_ref, got_ref)


def hop_kernel(half, start_ref, high_ref, low_ref, got_ref, after_ref, out_ref):
    zero, one = split(got_ref[:, :half]), split(got_ref[:, half:])

    def chain(at):
        rows = slice(at * half, (at + 1) * half)
        return high_ref[rows, :], low_ref[rows, :]

    out_ref[:, :half] = start_ref[:, :half] + product(zero, chain(0))
    out_ref[:, half:] = (
        start_ref[:, half:] + product(zero, chain(1)) + product(one, chain(2))
    )


def sweep_kernel(
    half, matrix_ref, up_ref, state_ref, seen_ref, factor_ref, straddle_ref, wide_ref, out_ref
):
    columns = matrix_ref.shape[1]
    reach = columns + half
    low_lanes, high_lanes = slice(0, half), slice(half, None)
    outer = split(state_ref[:, 0:half])
    coeffs = split(state_ref[:, half : 2 * half])
    back = split(state_ref[:, 2 * half :])
    begun = split(up_ref[...])
    reached = factor_ref[3]
    inside = stack(seen_ref[...] - product(begun, reached), -reached)
    next_outer = split(stack(product(begun, factor_ref[0]), factor_ref[0]))
    next_coeffs = split(product(inside, factor_ref[2]))
    current = jnp.transpose(matrix_ref[...])
    straddle, aligned = split(straddle_ref[0]), split(wide_ref[0])
    change = beside(
        product(coeffs, cut(aligned, lanes=low_lanes))
        + product(back, cut(straddle, lanes=low_lanes)),
        product(outer, cut(straddle, lanes=high_lanes))
        + product(coeffs, cut(aligned, lanes=high_lanes)),
    )
    straddle, aligned = split(straddle_ref[1]), split(wide_ref[1])
    later = beside(
        product(next_coeffs, cut(aligned, lanes=low_lanes)),
        product(next_outer, cut(straddle, lanes=high_lanes))
        + product(next_coeffs, cut(aligned, lanes=high_lanes)),
    )
    out_ref[:columns, :] = current - change[:columns] - later[:columns]
    out_ref[columns:reach, :] = -change[columns:] - later[columns:reach]
    out_ref[reach:, :] = -later[reach:]


def response_kernel(
    half, index_ref, own_ref, got_ref, up_ref, local_ref, factor_ref, straddle_ref,
    base_ref, high_ref, low_ref,
):
    columns = base_ref.shape[0]
    reach = columns + half
    keep = jnp.where(index_ref[2] == 0, 1.0, 0.0)
    first_rows = slice(3 * half, 3 * half + columns)
    first = stack(own_ref[first_rows, :], own_ref[0:half, :])
    offset = product(first, keep * up_ref[columns:, :])
    summed = stack(
        own_ref[3 * half + columns :, :] + offset[:columns] + keep * up_ref[:columns, :],
        own_ref[half : 2 * half, :] + offset[columns:],
        own_ref[2 * half : 3 * half, :],
    )
    back = product(summed, factor_ref[1])
    change = product(back, straddle_ref[1][:, :half])
    local = beside(local_ref[:, :half] - change, local_ref[:, half:])
    base, middle, last = local[:columns], local[columns:reach], local[reach:]

    def store(at, value):
        high, low = split(value)
        high_ref[at * half : (at + 1) * half, :] = high
        low_ref[at * half : (at + 1) * half, :] = low

    @pl.when(index_ref[0] != 0)
    def _():
        base_ref[...] = base
        store(0, middle)
        store(1, last)

    @pl.when(index_ref[0] == 0)
    def _():
        middle_pair, last_pair = split(middle), split(last)
        zero = stack(got_ref[first_rows, :], got_ref[0:half, :])
        one = stack(got_ref[3 * half + columns :, :], got_ref[half : 3 * half, :])
        after_zero = product(zero, middle_pair)
        after_one = product(one, last_pair)
        base_ref[...] = base + after_zero[:columns] + after_one[:columns]
        store(0, after_zero[columns:] + after_one[columns:reach])
        store(1, after_one[reach:])


def final_kernel(index_ref, own_ref, got_ref, base_ref, high_ref, low_ref, out_ref):
    def body(even_ref, odd_ref):
        carry = stack(even_ref[...], odd_ref[...])
        reply = high_ref[...], low_ref[...]
        out_ref[...] = jnp.transpose(base_ref[...] + product(carry, reply))

    by_core(index_ref, body, own_ref, got_ref)


def call(body, outs, *operands, flops=0, free=()):
    space = pl.BlockSpec(memory_space=pltpu.VMEM)
    specs = []
    for at, operand in enumerate(operands):
        if operand.dtype == jnp.int32:
            specs.append(pl.BlockSpec(memory_space=pltpu.SMEM))
        else:
            specs.append(pl.BlockSpec(memory_space=pl.ANY) if at in free else space)
    shapes = [
        shape if isinstance(shape, jax.ShapeDtypeStruct) else jax.ShapeDtypeStruct(shape, F32)
        for shape in outs
    ]
    moved = sum(4 * operand.size for operand in operands) + sum(4 * shape.size for shape in shapes)
    return pl.pallas_call(
        body,
        out_shape=shapes,
        in_specs=specs,
        out_specs=[space] * len(shapes),
        compiler_params=pltpu.CompilerParams(vmem_limit_bytes=VMEM_GRANT),
        cost_estimate=pl.CostEstimate(flops=flops, bytes_accessed=moved, transcendentals=0),
    )(*operands)


def gathered(shard, axis):
    count = lax.axis_size(axis)
    me = lax.axis_index(axis)
    every = ((0, 0), (1, 1))
    power = count & (count - 1) == 0
    arrays, places, layout = [shard], [me], [every]
    for step in range(1, count):
        route = [(i ^ step if power else (i + step) % count, i) for i in range(count)]
        arrays.append(lax.ppermute(shard, axis, route))
        places.append(me ^ step if power else (me + step) % count)
        layout.append(every)
    return arrays, places, layout


def on_device(eigenvectors, aligned_vectors, straddle_vectors):
    aligned = jnp.swapaxes(aligned_vectors, 1, 2)
    straddle = jnp.swapaxes(straddle_vectors, 1, 2)
    sweeps, width, span = aligned.shape
    half = span // 2
    columns = eigenvectors.shape[1]
    part = columns // 2
    rows = lax.axis_size("row")
    row = lax.axis_index("row")
    chips = rows // 2

    straddle_parts, places, layout = gathered(straddle, "col")
    aligned_parts, _, _ = gathered(aligned, "col")
    parity = row % 2
    outside = jnp.where(parity == 0, row == 0, row == rows - 1)
    index = jnp.stack(
        [parity, outside.astype(jnp.int32), (row == 0).astype(jnp.int32), row]
        + [jnp.asarray(place, jnp.int32) for place in places]
    ).astype(jnp.int32)
    unit = 2 * half * half * half * 3
    message = (half + PAD + columns, half)
    reach = columns + half

    wide_straddle, inner, outer = call(
        functools.partial(gram_kernel, layout, width, half),
        [(sweeps, half, span), message, message],
        index, *straddle_parts, eigenvectors, flops=5 * unit,
    )
    inside_route = [(i, i ^ 1) for i in range(rows)]
    outside_route = [(i, (i - 1 if i % 2 == 0 else i + 1) % rows) for i in range(rows)]
    outer_got = lax.ppermute(outer, "row", outside_route)
    inner_got = lax.ppermute(inner, "row", inside_route)
    wide_aligned, step, up, state, seen, _, factor = call(
        functools.partial(local_kernel, layout, width, half),
        [
            (sweeps, half, span), (3 * half + 2 * columns, half), (reach, half), (reach, 3 * half),
            (reach, half), (2, 2, half, half), (4, half, half),
        ],
        index, *aligned_parts, eigenvectors, wide_straddle, inner, inner_got, outer, outer_got,
        flops=100 * unit,
    )
    step_got = lax.ppermute(step, "row", inside_route)
    up_got = lax.ppermute(up, "row", [(i, i + 1) for i in range(rows - 1)])
    halves = jax.ShapeDtypeStruct((3 * half, half), BF16)
    high, low, start = call(
        functools.partial(compose_kernel, half),
        [halves, halves, (part, span)],
        index, step, step_got, flops=6 * unit,
    )
    down = [(i, i - 2) for i in range(2, rows)]
    local = base = None

    def shadow(local, base):
        if local is None:
            (local,) = call(
                functools.partial(sweep_kernel, half), [(reach + half, span)],
                eigenvectors, up, state, seen, factor, wide_straddle, wide_aligned,
                flops=20 * unit,
            )
            return local, None, (), local
        wide_halves = jax.ShapeDtypeStruct((span, span), BF16)
        base, *reply = call(
            functools.partial(response_kernel, half),
            [(columns, span), wide_halves, wide_halves],
            index, step, step_got, up_got, local, factor, wide_straddle, flops=20 * unit,
        )
        return local, base, reply, base

    carry, reply, got = start, (), jnp.zeros_like(start)
    for hop in range(chips - 1):
        got = lax.ppermute(carry, "row", down)
        after = start
        if base is None:
            local, base, reply, after = shadow(local, base)
        if hop < chips - 2:
            (carry,) = call(
                functools.partial(hop_kernel, half), [(part, span)],
                start, high, low, got, after, flops=unit, free=(4,),
            )
    while base is None:
        local, base, reply, after = shadow(local, base)
    other = lax.ppermute(got, "row", inside_route)
    (result,) = call(
        final_kernel, [(span, columns)], index, got, other, base, *reply, flops=4 * unit
    )
    return result


def solution(mesh):
    placed = (P("row", "col"), P(None, "row", "col"), P(None, "row", "col"))

    return jax.shard_map(
        on_device, mesh=mesh, in_specs=placed, out_specs=P("row", "col"), check_vma=False
    )
```

time: 105 us -> 77.1 us (0.73)
  Pallas kernels: 39.3 us -> 20.8 us
  local copies, waits for them, and re-layouts: 7.59 us -> 1.99 us
  starting transfers between devices: 21.1 us -> 18.3 us
    pallas_call x7 -> x8, Pallas kernels: 39.3 us -> 20.8 us  [call(): pl.pallas_call(body, out_shape=shapes, in_specs=specs, out_specs=[space]...]
    unnamed x40 -> x8, local copies, waits for them, and re-layouts: 5.19 us -> 1.91 us
    ppermute x8 -> x6, starting transfers between devices: 11.2 us -> 7.98 us  [gathered(): arrays.append(lax.ppermute(shard, axis, route))]
    ppermute x1, waiting for transfers between devices: 2.86 us -> 0.23 us  [on_device(): step_got = lax.ppermute(step, 'row', inside_route)]
    ppermute x8 -> x6, waiting for transfers between devices: 18.7 us -> 21.1 us  [gathered(): arrays.append(lax.ppermute(shard, axis, route))]
    slice x6 -> x0, local copies, waits for them, and re-layouts: 1.72 us -> none  [the longest x1 0.85 us: on_device(): wide_aligned[1:]]
    ppermute x1, waiting for transfers between devices: 0.01 us -> 1.35 us  [on_device(): other = lax.ppermute(got, 'row', inside_route)]
    ppermute x3, waiting for transfers between devices: 14.1 us -> 13 us  [on_device(): got = lax.ppermute(carry, 'row', down)]
  transfers between devices with their start and end apart: 16 -> 14, of which waited for: 12 -> 10; matrix products, arithmetic and copies ran while one was open for 2% -> 0% of each run, Pallas kernels for 11% -> 9%
where the time goes in v1:
time: 77.1 us; the launch traced here: 76.9 us
  waiting for transfers between devices  35.7 us (46%)
  Pallas kernels  20.8 us (27%)
  starting transfers between devices  18.3 us (24%)
  local copies, waits for them, and re-layouts  1.99 us (3%)
    ppermute x6, waiting for transfers between devices, gathered(): arrays.append(lax.ppermute(shard, axis, route))  21.1 us
    pallas_call x8, Pallas kernels, call(): pl.pallas_call(body, out_shape=shapes, in_specs=specs, out_specs=[space]...  20.8 us
    ppermute x3, waiting for transfers between devices, on_device(): got = lax.ppermute(carry, 'row', down)  13 us
    ppermute x6, starting transfers between devices, gathered(): arrays.append(lax.ppermute(shard, axis, route))  7.98 us
    ppermute x3, starting transfers between devices, on_device(): got = lax.ppermute(carry, 'row', down)  4.04 us
    ppermute x1, starting transfers between devices, on_device(): outer_got = lax.ppermute(outer, 'row', outside_route)  3.7 us
    ppermute x1, starting transfers between devices, on_device(): up_got = lax.ppermute(up, 'row', [(i, i + 1) for i in range(rows - 1)])  2.41 us
    unnamed x8, local copies, waits for them, and re-layouts  1.91 us
  transfers between devices with their start and end apart: 14, of which 10 were waited for; matrix products, arithmetic and copies ran while one was open for 0% of the time, Pallas kernels for 9%

profile of v1, /device:TPU:0, one launch (start us, length us, event | category | flops | bytes accessed | tf_op | source)
XLA Modules:
  0.0 76.9 jit_solution(1583730651152669179)
XLA Ops:
  0.0 3.9 %collective-permute-start.5 = (f32[2,64,512]{2,1,0:T(8,128)}, f32[2,64,512]{2,1,0:T(8,128)S(1)}, u32[]{:S(2)}, u32[]{:S(2)}) collective-permute-start(f32[2,64,512]{2,1,0:T(8,128)} %bitcast.10), channel_id=1, source_target_pairs={{3,0},{2,1},{1,2},{0,3},{7,4},{6,5},{5,6},{4,7},{11,8},{10,9},{9,1... | collective-permute-start | bytes 786440 | tf_op jit(solution)/shard_map/ppermute | solution.py:449
  3.9 0.5 collective-permute-start.4
  4.5 0.1 stack.43.index_ref
  4.6 6.8 %collective-permute-done.5.refs_3_ = f32[2,64,512]{2,1,0:T(8,128)S(1)} collective-permute-done((f32[2,64,512]{2,1,0:T(8,128)}, f32[2,64,512]{2,1,0:T(8,128)S(1)}, u32[]{:S(2)}, u32[]{:S(2)}) %collective-permute-start.5) | collective-permute-done | bytes 262176 | tf_op jit(solution)/shard_map/ppermute | solution.py:449
  11.3 4.7 %collective-permute-done.4.refs_2_ = f32[2,64,512]{2,1,0:T(8,128)S(1)} collective-permute-done((f32[2,64,512]{2,1,0:T(8,128)}, f32[2,64,512]{2,1,0:T(8,128)S(1)}, u32[]{:S(2)}, u32[]{:S(2)}) %collective-permute-start.4) | collective-permute-done | bytes 262176 | tf_op jit(solution)/shard_map/ppermute | solution.py:449
  16.1 0.3 collective-permute-done.3.refs_1_
  16.4 0.9 %copy-done = f32[2,512,64]{1,2,0:T(8,128)S(1)} copy-done((f32[2,512,64]{1,2,0:T(8,128)S(1)}, f32[2,512,64]{1,2,0:T(8,128)}, u32[]{:S(2)}) %copy-start) | copy-done | bytes 262168
  17.3 0.9 %copy-done.2 = f32[512,128]{1,0:T(8,128)S(1)} copy-done((f32[512,128]{1,0:T(8,128)S(1)}, f32[512,128]{1,0:T(8,128)}, u32[]{:S(2)}) %copy-start.2) | copy-done | bytes 262168
  18.3 1.4 %shard_map.37 = (f32[2,256,512]{2,1,0:T(8,128)S(1)}, f32[392,256]{1,0:T(8,128)S(1)}, f32[392,256]{1,0:T(8,128)S(1)}) custom-call(s32[8]{0:T(128)S(1)} %stack.43.index_ref, f32[2,64,512]{2,1,0:T(8,128)S(1)} %bitcast.13, f32[2,64,512]{2,1,0:T(8,128)S(1)} %collective-permute-done.3.refs_1_, f32[2,64,512]{2,1,0:T(8,128)S(1)} %collective-permute-done.4.refs_2_, ...), custom_call_target="tpu_custom_call" | custom-call | flops 503316480 | bytes 3162144 | tf_op jit(solution)/shard_map/pallas_call | solution.py:431
  19.6 0.1 collective-permute-start.6
  19.7 3.7 %collective-permute-start.7 = (f32[392,256]{1,0:T(8,128)S(1)}, f32[392,256]{1,0:T(8,128)S(1)}, u32[]{:S(2)}, u32[]{:S(2)}) collective-permute-start(f32[392,256]{1,0:T(8,128)S(1)} %get-tuple-element.22.refs_8_), channel_id=1, source_target_pairs={{0,28},{4,8},{8,4},{12,16},{16,12},{20,24},{24,20},{28,0},{1,29},{... | collective-permute-start | bytes 1204232 | tf_op jit(solution)/shard_map/ppermute | solution.py:485
  23.4 1.7 %collective-permute-start.2 = (f32[2,64,512]{2,1,0:T(8,128)S(1)}, f32[2,64,512]{2,1,0:T(8,128)S(1)}, u32[]{:S(2)}, u32[]{:S(2)}) collective-permute-start(f32[2,64,512]{2,1,0:T(8,128)S(1)} %bitcast.14), channel_id=1, source_target_pairs={{3,0},{2,1},{1,2},{0,3},{7,4},{6,5},{5,6},{4,7},{11,8},{10,9},{9,1... | collective-permute-start | bytes 786440 | tf_op jit(solution)/shard_map/ppermute | solution.py:449
  25.1 1.3 %collective-permute-start.1 = (f32[2,64,512]{2,1,0:T(8,128)S(1)}, f32[2,64,512]{2,1,0:T(8,128)S(1)}, u32[]{:S(2)}, u32[]{:S(2)}) collective-permute-start(f32[2,64,512]{2,1,0:T(8,128)S(1)} %bitcast.15), channel_id=1, source_target_pairs={{2,0},{3,1},{0,2},{1,3},{6,4},{7,5},{4,6},{5,7},{10,8},{11,9},{8,1... | collective-permute-start | bytes 786440 | tf_op jit(solution)/shard_map/ppermute | solution.py:449
  26.4 0.5 collective-permute-start
  26.9 6.5 %collective-permute-done.2.refs_3_ = f32[2,64,512]{2,1,0:T(8,128)S(1)} collective-permute-done((f32[2,64,512]{2,1,0:T(8,128)S(1)}, f32[2,64,512]{2,1,0:T(8,128)S(1)}, u32[]{:S(2)}, u32[]{:S(2)}) %collective-permute-start.2) | collective-permute-done | bytes 262176 | tf_op jit(solution)/shard_map/ppermute | solution.py:449
  33.4 2.8 %collective-permute-done.1.refs_2_ = f32[2,64,512]{2,1,0:T(8,128)S(1)} collective-permute-done((f32[2,64,512]{2,1,0:T(8,128)S(1)}, f32[2,64,512]{2,1,0:T(8,128)S(1)}, u32[]{:S(2)}, u32[]{:S(2)}) %collective-permute-start.1) | collective-permute-done | bytes 262176 | tf_op jit(solution)/shard_map/ppermute | solution.py:449
  36.2 10.6 %shard_map.38 = (f32[2,256,512]{2,1,0:T(8,128)S(1)}, f32[1024,256]{1,0:T(8,128)S(1)}, f32[384,256]{1,0:T(8,128)S(1)}, f32[384,768]{1,0:T(8,128)S(1)}, f32[384,25...) custom-call(s32[8]{0:T(128)S(1)} %stack.43.index_ref, f32[2,64,512]{2,1,0:T(8,128)S(1)} %bitcast.17, ...), custom_call_target="tpu_custom_call" | custom-call | flops 10066329600 | bytes 10125344 | tf_op jit(solution)/shard_map/pallas_call | solution.py:431
  46.9 2.4 %collective-permute-start.11 = (f32[384,256]{1,0:T(8,128)S(1)}, f32[384,256]{1,0:T(8,128)S(1)}, u32[]{:S(2)}, u32[]{:S(2)}) collective-permute-start(f32[384,256]{1,0:T(8,128)S(1)} %get-tuple-element.27.up_ref), channel_id=1, source_target_pairs={{0,4},{4,8},{8,12},{12,16},{16,20},{20,24},{24,28},{1,5},{5,9},{9,... | collective-permute-start | bytes 1179656 | tf_op jit(solution)/shard_map/ppermute | solution.py:497
  49.3 0.2 collective-permute-done.8.got_ref
  49.5 1.4 %shard_map.39 = (bf16[768,256]{1,0:T(8,128)(2,1)S(1)}, bf16[768,256]{1,0:T(8,128)(2,1)S(1)}, f32[64,512]{1,0:T(8,128)S(1)}) custom-call(s32[8]{0:T(128)S(1)} %stack.43.index_ref, f32[1024,256]{1,0:T(8,128)S(1)} %get-tuple-element.23.own_ref, f32[1024,256]{1,0:T(8,128)S(1)} %collective-permute-done.8.got_ref), custom_call_target="tpu_custom_call" | custom-call | flops 603979776 | bytes 3801120 | tf_op jit(solution)/shard_map/pallas_call | solution.py:431
  50.9 1.5 %collective-permute-start.9 = (f32[64,512]{1,0:T(8,128)S(1)}, f32[64,512]{1,0:T(8,128)S(1)}, u32[]{:S(2)}, u32[]{:S(2)}) collective-permute-start(f32[64,512]{1,0:T(8,128)S(1)} %get-tuple-element.24.start_ref), channel_id=1, source_target_pairs={{8,0},{12,4},{16,8},{20,12},{24,16},{28,20},{9,1},{13,5},{17,9},{2... | collective-permute-start | bytes 393224 | tf_op jit(solution)/shard_map/ppermute | solution.py:525
  52.4 2.2 %shard_map.40.after_ref.local_ref = f32[640,512]{1,0:T(8,128)S(1)} custom-call(f32[512,128]{1,0:T(8,128)S(1)} %copy-done.3, f32[384,256]{1,0:T(8,128)S(1)} %get-tuple-element.27.up_ref, f32[384,768]{1,0:T(8,128)S(1)} %get-tuple-element.28.state_ref, f32[384,256]{1,0:T(8,128)S(1)} %get-tuple-element.29.seen_ref, ...), custom_call_target="tpu_custom_call" | custom-call | flops 2013265920 | bytes 6684672 | tf_op jit(solution)/shard_map/pallas_call | solution.py:431
  54.6 4.4 %collective-permute-done.9.got_ref = f32[64,512]{1,0:T(8,128)S(1)} collective-permute-done((f32[64,512]{1,0:T(8,128)S(1)}, f32[64,512]{1,0:T(8,128)S(1)}, u32[]{:S(2)}, u32[]{:S(2)}) %collective-permute-start.9) | collective-permute-done | bytes 131104 | tf_op jit(solution)/shard_map/ppermute | solution.py:525
  59.0 0.3 shard_map.41
  59.3 1.3 %collective-permute-start.10 = (f32[64,512]{1,0:T(8,128)S(1)}, f32[64,512]{1,0:T(8,128)S(1)}, u32[]{:S(2)}, u32[]{:S(2)}) collective-permute-start(f32[64,512]{1,0:T(8,128)S(1)} %shard_map.41), channel_id=1, source_target_pairs={{8,0},{12,4},{16,8},{20,12},{24,16},{28,20},{9,1},{13,5},{17,9},{2... | collective-permute-start | bytes 393224 | tf_op jit(solution)/shard_map/ppermute | solution.py:525
  60.6 2.9 %shard_map.42 = (f32[128,512]{1,0:T(8,128)S(1)}, bf16[512,512]{1,0:T(8,128)(2,1)S(1)}, bf16[512,512]{1,0:T(8,128)(2,1)S(1)}) custom-call(s32[8]{0:T(128)S(1)} %stack.43.index_ref, f32[1024,256]{1,0:T(8,128)S(1)} %get-tuple-element.23.own_ref, f32[1024,256]{1,0:T(8,128)S(1)} %collective-permute-done.8.got_ref, f32[384,256]{1,0:T(8,128)S(1)} %collective-permute-done.11.up_ref, ...), custom_call_target="tpu_custom_call" | custom-call | flops 2013265920 | bytes 8257568 | tf_op jit(solution)/shard_map/pallas_call | solution.py:431
  63.5 3.1 %collective-permute-done.10.got_ref = f32[64,512]{1,0:T(8,128)S(1)} collective-permute-done((f32[64,512]{1,0:T(8,128)S(1)}, f32[64,512]{1,0:T(8,128)S(1)}, u32[]{:S(2)}, u32[]{:S(2)}) %collective-permute-start.10) | collective-permute-done | bytes 131104 | tf_op jit(solution)/shard_map/ppermute | solution.py:525
  66.6 0.3 shard_map.43
  66.9 1.3 %collective-permute-start.12 = (f32[64,512]{1,0:T(8,128)S(1)}, f32[64,512]{1,0:T(8,128)S(1)}, u32[]{:S(2)}, u32[]{:S(2)}) collective-permute-start(f32[64,512]{1,0:T(8,128)S(1)} %shard_map.43), channel_id=1, source_target_pairs={{8,0},{12,4},{16,8},{20,12},{24,16},{28,20},{9,1},{13,5},{17,9},{2... | collective-permute-start | bytes 393224 | tf_op jit(solution)/shard_map/ppermute | solution.py:525
  68.2 5.6 %collective-permute-done.12.own_ref = f32[64,512]{1,0:T(8,128)S(1)} collective-permute-done((f32[64,512]{1,0:T(8,128)S(1)}, f32[64,512]{1,0:T(8,128)S(1)}, u32[]{:S(2)}, u32[]{:S(2)}) %collective-permute-start.12) | collective-permute-done | bytes 131104 | tf_op jit(solution)/shard_map/ppermute | solution.py:525
  73.8 1.3 %collective-permute-done.13.got_ref = f32[64,512]{1,0:T(8,128)S(1)} collective-permute-done((f32[64,512]{1,0:T(8,128)S(1)}, f32[64,512]{1,0:T(8,128)S(1)}, u32[]{:S(2)}, u32[]{:S(2)}) %collective-permute-start.13) | collective-permute-done | bytes 131104 | tf_op jit(solution)/shard_map/ppermute | solution.py:536
  75.1 1.7 %shard_map.44 = f32[512,128]{1,0:T(8,128)} custom-call(s32[8]{0:T(128)S(1)} %stack.43.index_ref, f32[64,512]{1,0:T(8,128)S(1)} %collective-permute-done.12.own_ref, f32[64,512]{1,0:T(8,128)S(1)} %collective-permute-done.13.got_ref, f32[128,512]{1,0:T(8,128)S(1)} %get-tuple-element.32.after_ref.base_ref, bf16[512,512]{1,0:T(8,128)(2,1)S(1)} %get-tuple-element.33.high_ref, ...), custom_call_target="tpu_custom_call" | custom-call | flops 402653184 | bytes 2883616 | tf_op jit(solution)/shard_map/pallas_call | solution.py:431
  (13 shorter events, 0.2 us)
Async XLA Ops:
  0.0 11.3 %collective-permute-start.5 = (f32[2,64,512]{2,1,0:T(8,128)}, f32[2,64,512]{2,1,0:T(8,128)S(1)}, u32[]{:S(2)}, u32[]{:S(2)}) collective-permute-start(f32[2,64,512]{2,1,0:T(8,128)} %bitcast.10), channel_id=1, source_target_pairs={{3,0},{2,1},{1,2},{0,3},{7,4},{6,5},{5,6},{4,7},{11,8},{10,9},{9,1... | collective-permute-start | bytes 786440 | tf_op jit(solution)/shard_map/ppermute | solution.py:449
  3.9 12.1 %collective-permute-start.4 = (f32[2,64,512]{2,1,0:T(8,128)}, f32[2,64,512]{2,1,0:T(8,128)S(1)}, u32[]{:S(2)}, u32[]{:S(2)}) collective-permute-start(f32[2,64,512]{2,1,0:T(8,128)} %bitcast.11), channel_id=1, source_target_pairs={{2,0},{3,1},{0,2},{1,3},{6,4},{7,5},{4,6},{5,7},{10,8},{11,9},{8,1... | collective-permute-start | bytes 786440 | tf_op jit(solution)/shard_map/ppermute | solution.py:449
  4.4 11.9 %collective-permute-start.3 = (f32[2,64,512]{2,1,0:T(8,128)}, f32[2,64,512]{2,1,0:T(8,128)S(1)}, u32[]{:S(2)}, u32[]{:S(2)}) collective-permute-start(f32[2,64,512]{2,1,0:T(8,128)} %bitcast.12), channel_id=1, source_target_pairs={{1,0},{0,1},{3,2},{2,3},{5,4},{4,5},{7,6},{6,7},{9,8},{8,9},{11,10... | collective-permute-start | bytes 786440 | tf_op jit(solution)/shard_map/ppermute | solution.py:449
  16.4 1.0 %copy-start = (f32[2,512,64]{1,2,0:T(8,128)S(1)}, f32[2,512,64]{1,2,0:T(8,128)}, u32[]{:S(2)}) copy-start(f32[2,512,64]{1,2,0:T(8,128)} %param.5) | copy-start | bytes 786436
  17.3 0.9 %copy-start.2 = (f32[512,128]{1,0:T(8,128)S(1)}, f32[512,128]{1,0:T(8,128)}, u32[]{:S(2)}) copy-start(f32[512,128]{1,0:T(8,128)} %matrix_ref.1) | copy-start | bytes 786436
  18.3 5.2 %copy-start.1 = (f32[2,512,64]{1,2,0:T(8,128)S(1)}, f32[2,512,64]{1,2,0:T(8,128)}, u32[]{:S(2)}) copy-start(f32[2,512,64]{1,2,0:T(8,128)} %param.4) | copy-start | bytes 786436
  18.3 18.0 %copy-start.3 = (f32[512,128]{1,0:T(8,128)S(1)}, f32[512,128]{1,0:T(8,128)}, u32[]{:S(2)}) copy-start(f32[512,128]{1,0:T(8,128)} %matrix_ref.1) | copy-start | bytes 786436
  19.6 16.6 %collective-permute-start.6 = (f32[392,256]{1,0:T(8,128)S(1)}, f32[392,256]{1,0:T(8,128)S(1)}, u32[]{:S(2)}, u32[]{:S(2)}) collective-permute-start(f32[392,256]{1,0:T(8,128)S(1)} %get-tuple-element.21.refs_6_), channel_id=1, source_target_pairs={{0,4},{4,0},{8,12},{12,8},{16,20},{20,16},{24,28},{28,24},{1,5},{5... | collective-permute-start | bytes 1204232 | tf_op jit(solution)/shard_map/ppermute | solution.py:486
  19.7 16.5 %collective-permute-start.7 = (f32[392,256]{1,0:T(8,128)S(1)}, f32[392,256]{1,0:T(8,128)S(1)}, u32[]{:S(2)}, u32[]{:S(2)}) collective-permute-start(f32[392,256]{1,0:T(8,128)S(1)} %get-tuple-element.22.refs_8_), channel_id=1, source_target_pairs={{0,28},{4,8},{8,4},{12,16},{16,12},{20,24},{24,20},{28,0},{1,29},{... | collective-permute-start | bytes 1204232 | tf_op jit(solution)/shard_map/ppermute | solution.py:485
  23.4 10.0 %collective-permute-start.2 = (f32[2,64,512]{2,1,0:T(8,128)S(1)}, f32[2,64,512]{2,1,0:T(8,128)S(1)}, u32[]{:S(2)}, u32[]{:S(2)}) collective-permute-start(f32[2,64,512]{2,1,0:T(8,128)S(1)} %bitcast.14), channel_id=1, source_target_pairs={{3,0},{2,1},{1,2},{0,3},{7,4},{6,5},{5,6},{4,7},{11,8},{10,9},{9,1... | collective-permute-start | bytes 786440 | tf_op jit(solution)/shard_map/ppermute | solution.py:449
  25.1 11.1 %collective-permute-start.1 = (f32[2,64,512]{2,1,0:T(8,128)S(1)}, f32[2,64,512]{2,1,0:T(8,128)S(1)}, u32[]{:S(2)}, u32[]{:S(2)}) collective-permute-start(f32[2,64,512]{2,1,0:T(8,128)S(1)} %bitcast.15), channel_id=1, source_target_pairs={{2,0},{3,1},{0,2},{1,3},{6,4},{7,5},{4,6},{5,7},{10,8},{11,9},{8,1... | collective-permute-start | bytes 786440 | tf_op jit(solution)/shard_map/ppermute | solution.py:449
  26.4 9.8 %collective-permute-start = (f32[2,64,512]{2,1,0:T(8,128)S(1)}, f32[2,64,512]{2,1,0:T(8,128)S(1)}, u32[]{:S(2)}, u32[]{:S(2)}) collective-permute-start(f32[2,64,512]{2,1,0:T(8,128)S(1)} %bitcast.16), channel_id=1, source_target_pairs={{1,0},{0,1},{3,2},{2,3},{5,4},{4,5},{7,6},{6,7},{9,8},{8,9},{11,10... | collective-permute-start | bytes 786440 | tf_op jit(solution)/shard_map/ppermute | solution.py:449
  46.8 2.7 %collective-permute-start.8 = (f32[1024,256]{1,0:T(8,128)S(1)}, f32[1024,256]{1,0:T(8,128)S(1)}, u32[]{:S(2)}, u32[]{:S(2)}) collective-permute-start(f32[1024,256]{1,0:T(8,128)S(1)} %get-tuple-element.23.own_ref), channel_id=1, source_target_pairs={{0,4},{4,0},{8,12},{12,8},{16,20},{20,16},{24,28},{28,24},{1,5},{5... | collective-permute-start | bytes 3145736 | tf_op jit(solution)/shard_map/ppermute | solution.py:496
  46.9 13.7 %collective-permute-start.11 = (f32[384,256]{1,0:T(8,128)S(1)}, f32[384,256]{1,0:T(8,128)S(1)}, u32[]{:S(2)}, u32[]{:S(2)}) collective-permute-start(f32[384,256]{1,0:T(8,128)S(1)} %get-tuple-element.27.up_ref), channel_id=1, source_target_pairs={{0,4},{4,8},{8,12},{12,16},{16,20},{20,24},{24,28},{1,5},{5,9},{9,... | collective-permute-start | bytes 1179656 | tf_op jit(solution)/shard_map/ppermute | solution.py:497
  50.9 8.1 %collective-permute-start.9 = (f32[64,512]{1,0:T(8,128)S(1)}, f32[64,512]{1,0:T(8,128)S(1)}, u32[]{:S(2)}, u32[]{:S(2)}) collective-permute-start(f32[64,512]{1,0:T(8,128)S(1)} %get-tuple-element.24.start_ref), channel_id=1, source_target_pairs={{8,0},{12,4},{16,8},{20,12},{24,16},{28,20},{9,1},{13,5},{17,9},{2... | collective-permute-start | bytes 393224 | tf_op jit(solution)/shard_map/ppermute | solution.py:525
  59.3 7.2 %collective-permute-start.10 = (f32[64,512]{1,0:T(8,128)S(1)}, f32[64,512]{1,0:T(8,128)S(1)}, u32[]{:S(2)}, u32[]{:S(2)}) collective-permute-start(f32[64,512]{1,0:T(8,128)S(1)} %shard_map.41), channel_id=1, source_target_pairs={{8,0},{12,4},{16,8},{20,12},{24,16},{28,20},{9,1},{13,5},{17,9},{2... | collective-permute-start | bytes 393224 | tf_op jit(solution)/shard_map/ppermute | solution.py:525
  66.9 6.9 %collective-permute-start.12 = (f32[64,512]{1,0:T(8,128)S(1)}, f32[64,512]{1,0:T(8,128)S(1)}, u32[]{:S(2)}, u32[]{:S(2)}) collective-permute-start(f32[64,512]{1,0:T(8,128)S(1)} %shard_map.43), channel_id=1, source_target_pairs={{8,0},{12,4},{16,8},{20,12},{24,16},{28,20},{9,1},{13,5},{17,9},{2... | collective-permute-start | bytes 393224 | tf_op jit(solution)/shard_map/ppermute | solution.py:525
  73.8 1.3 %collective-permute-start.13 = (f32[64,512]{1,0:T(8,128)S(1)}, f32[64,512]{1,0:T(8,128)S(1)}, u32[]{:S(2)}, u32[]{:S(2)}) collective-permute-start(f32[64,512]{1,0:T(8,128)S(1)} %collective-permute-done.12.own_ref), channel_id=1, source_target_pairs={{0,4},{4,0},{8,12},{12,8},{16,20},{20,16},{24,28},{28,24},{1,5},{5... | collective-permute-start | bytes 393224 | tf_op jit(solution)/shard_map/ppermute | solution.py:536

commit v2 on v1

v2 whole, which is shorter than its diff:
```python
import functools

import jax
import jax.numpy as jnp
from jax import lax
from jax.experimental import pallas as pl
from jax.experimental.pallas import tpu as pltpu
from jax.sharding import PartitionSpec as P


F32 = jnp.float32
BF16 = jnp.bfloat16
BASE_BLOCK = 32
LANES = 128
PAD = 8
VMEM_GRANT = 16 * 1024 * 1024


def split(value):
    high = value.astype(BF16)
    return high, (value - high.astype(F32)).astype(BF16)


def raw_dot(left, right, transposed):
    dims = (((1,), (1 if transposed else 0,)), ((), ()))
    return lax.dot_general(left, right, dims, preferred_element_type=F32)


def product(left, right, transposed=False):
    left = left if isinstance(left, tuple) else split(left)
    right = right if isinstance(right, tuple) else split(right)
    return (
        raw_dot(left[0], right[0], transposed)
        + raw_dot(left[0], right[1], transposed)
        + raw_dot(left[1], right[0], transposed)
    )


def cut(pair, rows=slice(None), lanes=slice(None)):
    return pair[0][rows, lanes], pair[1][rows, lanes]


def stack(*values):
    return jnp.concatenate(values, axis=0)


def beside(*values):
    return jnp.concatenate(values, axis=1)


def block_inverse(packed, base):
    done = []
    for start in range(0, packed.shape[1], LANES):
        entries = packed[:, start : start + LANES]
        rows = lax.broadcasted_iota(jnp.int32, entries.shape, 0)
        lanes = lax.broadcasted_iota(jnp.int32, entries.shape, 1)
        group = (lanes // base) * base
        value = jnp.where(rows == lanes - group, 1.0, 0.0).astype(F32)
        for step in range(base - 1):
            top = (step // 8) * 8
            factor = jnp.take_along_axis(entries[top:], (group + step)[top:], axis=1)
            changed = value[top:] - factor * value[step : step + 1]
            value = stack(value[:top], changed) if top else changed
        done.append(value)
    return beside(*done)


def small_inverse(strict, across, base):
    order = strict.shape[0]
    lanes = lax.broadcasted_iota(jnp.int32, (base, order), 1) // base
    packed = jnp.zeros((base, order), F32)
    for block in range(order // base):
        packed = jnp.where(lanes == block, strict[block * base : (block + 1) * base], packed)
    solved = block_inverse(packed * across, base)
    return stack(*[jnp.where(lanes == block, solved, 0.0) for block in range(order // base)])


def lower_inverses(stricts, diagonals):
    order = stricts[0].shape[0]
    base = min(BASE_BLOCK, order)
    rows = lax.broadcasted_iota(jnp.int32, (order, order), 0)
    lanes = lax.broadcasted_iota(jnp.int32, (order, order), 1)
    result = []
    for strict, diagonal in zip(stricts, diagonals):
        across = 2.0 / diagonal
        along = jnp.sum(jnp.where(rows == lanes, across, 0.0), axis=1, keepdims=True)
        result.append(small_inverse(strict, across, base) * along)
    size = base
    while 2 * size < order:
        here = (rows // (2 * size) == lanes // (2 * size)) & (rows // size != lanes // size)
        wholes = [split(now) for now in result]
        starts = range(0, order, 2 * size)
        odds = [
            tuple(stack(*[part[at + size : at + 2 * size] for at in starts]) for part in whole)
            for whole in wholes
        ]
        inner = [
            product(odd, jnp.where(here, strict, 0.0)) for odd, strict in zip(odds, stricts)
        ]
        outer = [product(value, whole) for value, whole in zip(inner, wholes)]
        merged = []
        for now, change in zip(result, outer):
            bands = []
            for number, at in enumerate(starts):
                bands.append(now[at : at + size])
                bands.append(
                    now[at + size : at + 2 * size] - change[number * size : (number + 1) * size]
                )
            merged.append(stack(*bands))
        result = merged
        size *= 2
    if size < order:
        wholes = [split(now) for now in result]
        low, high = slice(0, size), slice(size, None)
        inner = [
            product(cut(whole, high, high), strict[high, low])
            for whole, strict in zip(wholes, stricts)
        ]
        outer = [product(value, cut(whole, low, low)) for value, whole in zip(inner, wholes)]
        result = [
            stack(now[low], beside(-change, now[high, high]))
            for now, change in zip(result, outer)
        ]
    return result


def core_now():
    return lax.axis_index("row") % 2


def chip_now():
    return lax.axis_index("row") // 2


def source_place(count, step):
    me = lax.axis_index("col")
    return me ^ step if count & (count - 1) == 0 else (me + step) % count


def place(layout, count, pieces, target):
    for (step, sweep), piece in zip(layout, pieces):
        width = piece.shape[1]
        start = pl.multiple_of(source_place(count, step) * width, width)
        for at in range(piece.shape[0]):
            target[sweep + at, pl.ds(start, width), :] = piece[at]


def triangle(order):
    rows = lax.broadcasted_iota(jnp.int32, (order, order), 0)
    lanes = lax.broadcasted_iota(jnp.int32, (order, order), 1)
    return rows > lanes, rows == lanes


def pack_grams(target, pair, below, diagonal):
    half = pair[0].shape[0]
    target[0:half, :] = jnp.where(below, pair[0], pair[1])
    for at, gram in enumerate(pair):
        target[half + at : half + at + 1, :] = jnp.sum(
            jnp.where(diagonal, gram, 0.0), axis=0, keepdims=True
        )


def first_kernel(matrix_ref, straddle_ref, aligned_ref, current_ref, own_ref, early_ref, late_ref):
    current_ref[...] = jnp.transpose(matrix_ref[...])
    own_ref[...] = straddle_ref[...]
    early_ref[...] = aligned_ref[0:1]
    late_ref[...] = aligned_ref[1:2]


def gram_kernel(layout, count, half, *refs):
    current_ref, wide_ref, inner_ref, outer_ref = refs[len(layout) :]
    place(layout, count, refs[: len(layout)], wide_ref)
    even = core_now() == 0
    below, diagonal = triangle(half)
    lows, highs = [], []
    for sweep in range(2):
        whole = split(wide_ref[sweep])
        low, high = cut(whole, lanes=slice(0, half)), cut(whole, lanes=slice(half, None))
        lows.append(product(low, low, True))
        highs.append(product(high, high, True))
        if sweep == 0:
            first = product(current_ref[:, half:], high, True)
    top = slice(half + PAD, None)
    inner_ref[top, :] = first
    outer_ref[top, :] = first
    pack_grams(inner_ref, [jnp.where(even, b, a) for a, b in zip(lows, highs)], below, diagonal)
    pack_grams(outer_ref, [jnp.where(even, a, b) for a, b in zip(lows, highs)], below, diagonal)


def keep_pairs(high_ref, low_ref, values):
    for at, value in enumerate(values):
        high_ref[at], low_ref[at] = split(value)


def between_kernel(half, current_ref, straddle_ref, high_ref, low_ref, raw_ref):
    whole = split(current_ref[...])
    upper, lower = cut(whole, lanes=slice(0, half)), cut(whole, lanes=slice(half, None))
    straddle = [split(straddle_ref[sweep]) for sweep in range(2)]
    bottom = [cut(value, lanes=slice(0, half)) for value in straddle]
    top = [cut(value, lanes=slice(half, None)) for value in straddle]
    keep_pairs(
        high_ref, low_ref, [product(top[0], top[1], True), product(bottom[0], bottom[1], True)]
    )
    raw_ref[0] = product(upper, bottom[0], True)
    raw_ref[1] = product(upper, bottom[1], True)
    raw_ref[2] = product(lower, top[1], True)


def aligned_kernel(layout, count, half, *refs):
    current_ref, straddle_ref, wide_ref, high_ref, low_ref, seen_ref = refs[len(layout) :]
    place(layout, count, refs[: len(layout)], wide_ref)
    below, diagonal = triangle(half)
    low_lanes, high_lanes = slice(0, half), slice(half, None)
    aligned = [split(wide_ref[sweep]) for sweep in range(2)]
    straddle = [split(straddle_ref[sweep]) for sweep in range(2)]
    bottom = [cut(value, lanes=low_lanes) for value in straddle]
    top = [cut(value, lanes=high_lanes) for value in straddle]
    first = [cut(value, lanes=low_lanes) for value in aligned]
    last = [cut(value, lanes=high_lanes) for value in aligned]
    grams = [product(value, value, True) for value in aligned]
    factors = lower_inverses(
        [jnp.where(below, gram, 0.0) for gram in grams],
        [jnp.sum(jnp.where(diagonal, gram, 0.0), axis=0, keepdims=True) for gram in grams],
    )
    whole = split(current_ref[...])
    seen_ref[0] = product(whole, aligned[0], True)
    seen_ref[1] = product(whole, aligned[1], True)
    through = [product(t, a, True) for t, a in zip(top, last)]
    onward = [product(a, b, True) for a, b in zip(first, bottom)]
    crosses = [
        product(aligned[0], aligned[1], True),
        product(bottom[0], first[1], True),
        product(top[0], last[1], True),
        product(last[0], top[1], True),
        product(first[0], bottom[1], True),
    ]
    leaving = [product(f, value) for f, value in zip(factors, onward)]
    keep_pairs(high_ref, low_ref, factors + leaving + through + crosses)


def local_kernel(
    columns, half, inner_ref, inner_got_ref, outer_ref, outer_got_ref,
    high_ref, low_ref, seen_ref, straddle_high_ref, straddle_low_ref, raw_ref,
    step_ref, up_ref, state_ref, sight_ref, factor_ref, square_ref,
):
    parity = core_now()
    below, _ = triangle(half)
    blank = jnp.zeros((half, half), F32)
    inner = inner_ref[0 : half + PAD, :] + inner_got_ref[0 : half + PAD, :]
    outer = outer_ref[0 : half + PAD, :] + outer_got_ref[0 : half + PAD, :]
    stricts, diagonals = [], []
    for packed in (inner, outer):
        mixed = packed[0:half]
        stricts.append(jnp.where(below, mixed, 0.0))
        stricts.append(jnp.where(below, jnp.transpose(mixed), 0.0))
        diagonals.append(packed[half : half + 1])
        diagonals.append(packed[half + 1 : half + 2])
    factors = lower_inverses(stricts, diagonals)

    def held(at):
        return high_ref[at], low_ref[at]

    factor_aligned, leaving, through = held(0), [held(2), held(3)], [held(4), held(5)]
    cross_aligned, cross_bottom_aligned, cross_top_aligned = held(6), held(7), held(8)
    cross_aligned_top, cross_aligned_bottom = held(9), held(10)
    cross_top = straddle_high_ref[0], straddle_low_ref[0]
    cross_bottom = straddle_high_ref[1], straddle_low_ref[1]
    for sweep in range(2):
        square_ref[sweep, parity] = factors[sweep]
        square_ref[sweep, 1 - parity] = factors[2 + sweep]
    factor_top = [split(square_ref[sweep, 0]) for sweep in range(2)]
    factor_bottom = split(square_ref[0, 1])
    rows = slice(half + PAD, None)
    own_first = inner_ref[rows, :]
    got_first = jnp.where(parity == 0, outer_got_ref[rows, :], inner_got_ref[rows, :])

    reached = [product(f, value) for f, value in zip(factor_top, through)]
    reached_pair = [split(value) for value in reached]
    own_pair = split(own_first)
    step1 = product(reached_pair[1], leaving[1])
    outer_coeff = stack(product(own_pair, factor_top[0]), square_ref[0, 0])
    inside = split(stack(seen_ref[0] - product(own_pair, reached_pair[0]), -reached[0]))
    carry0 = stack(raw_ref[0], blank) - product(inside, leaving[0])
    coeffs = product(inside, factor_aligned)
    back = product(stack(carry0[:columns] + got_first, carry0[columns:]), factor_bottom)
    outer_pair, coeff_pair, back_pair = split(outer_coeff), split(coeffs), split(back)
    begun = (
        stack(raw_ref[2], blank)
        - product(outer_pair, cross_top)
        - product(coeff_pair, cross_aligned_top)
    )
    sight = (
        stack(seen_ref[1], blank)
        - product(coeff_pair, cross_aligned)
        - product(outer_pair, cross_top_aligned)
        - product(back_pair, cross_bottom_aligned)
    )
    raw = (
        stack(raw_ref[1], blank)
        - product(coeff_pair, cross_aligned_bottom)
        - product(back_pair, cross_bottom)
    )
    carry1 = raw - product(sight, leaving[1]) + product(begun, step1)
    up_ref[...] = begun
    sight_ref[...] = sight
    state_ref[:, 0:half] = outer_coeff
    state_ref[:, half : 2 * half] = coeffs
    state_ref[:, 2 * half :] = back
    factor_ref[0] = square_ref[1, 0]
    factor_ref[1] = square_ref[1, 1]
    factor_ref[2] = reached[1]
    step_ref[0:half, :] = carry0[columns:]
    step_ref[half : 2 * half, :] = carry1[columns:]
    step_ref[2 * half : 3 * half, :] = step1
    step_ref[3 * half : 3 * half + columns, :] = carry0[:columns]
    step_ref[3 * half + columns :, :] = carry1[:columns]


def by_core(body, own_ref, got_ref):
    @pl.when(core_now() == 0)
    def _():
        body(own_ref, got_ref)

    @pl.when(core_now() != 0)
    def _():
        body(got_ref, own_ref)


def chain_parts(ref, half):
    return [split(ref[at * half : (at + 1) * half, :]) for at in range(3)]


def start_kernel(half, own_ref, got_ref, start_ref):
    part = start_ref.shape[0]

    def body(even_ref, odd_ref):
        even0, even_mix, even1 = chain_parts(even_ref, half)

        def rows(ref, sweep):
            first = pl.multiple_of(3 * half + 2 * sweep * part + core_now() * part, 8)
            return ref[pl.ds(first, part), :]

        odd_first = split(rows(odd_ref, 0))
        start_ref[:, :half] = rows(even_ref, 0) + product(odd_first, even0)
        start_ref[:, half:] = (
            rows(even_ref, 1) + product(odd_first, even_mix) + product(rows(odd_ref, 1), even1)
        )

    by_core(body, own_ref, got_ref)


def chain_kernel(half, own_ref, got_ref, high_ref, low_ref):
    def body(even_ref, odd_ref):
        even0, even_mix, even1 = chain_parts(even_ref, half)
        odd0, odd_mix, odd1 = chain_parts(odd_ref, half)
        keep_pairs(
            high_ref,
            low_ref,
            [
                product(odd0, even0),
                product(odd0, even_mix) + product(odd_mix, even1),
                product(odd1, even1),
            ],
        )

    by_core(body, own_ref, got_ref)


def hop_kernel(
    half, receiver, start_ref, high_ref, low_ref, got_ref, kept_ref, out_ref, keep_ref
):
    got = got_ref[...]
    zero, one = split(got[:, :half]), split(got[:, half:])

    def chain(at):
        return high_ref[at], low_ref[at]

    out_ref[:, :half] = start_ref[:, :half] + product(zero, chain(0))
    out_ref[:, half:] = (
        start_ref[:, half:] + product(zero, chain(1)) + product(one, chain(2))
    )
    keep_ref[...] = jnp.where(chip_now() == receiver, got, kept_ref[...])


def sweep_kernel(
    half, current_ref, up_ref, state_ref, sight_ref, factor_ref, high_ref, low_ref,
    straddle_ref, wide_ref, out_ref,
):
    columns = current_ref.shape[0]
    reach = columns + half
    low_lanes, high_lanes = slice(0, half), slice(half, None)
    outer = split(state_ref[:, 0:half])
    coeffs = split(state_ref[:, half : 2 * half])
    back = split(state_ref[:, 2 * half :])
    begun = split(up_ref[...])
    reached = factor_ref[2]
    inside = stack(sight_ref[...] - product(begun, reached), -reached)
    next_outer = split(stack(product(begun, factor_ref[0]), factor_ref[0]))
    next_coeffs = split(product(inside, (high_ref[1], low_ref[1])))
    current = current_ref[...]
    straddle, aligned = split(straddle_ref[0]), split(wide_ref[0])
    change = beside(
        product(coeffs, cut(aligned, lanes=low_lanes))
        + product(back, cut(straddle, lanes=low_lanes)),
        product(outer, cut(straddle, lanes=high_lanes))
        + product(coeffs, cut(aligned, lanes=high_lanes)),
    )
    straddle, aligned = split(straddle_ref[1]), split(wide_ref[1])
    later = beside(
        product(next_coeffs, cut(aligned, lanes=low_lanes)),
        product(next_outer, cut(straddle, lanes=high_lanes))
        + product(next_coeffs, cut(aligned, lanes=high_lanes)),
    )
    out_ref[:columns, :] = current - change[:columns] - later[:columns]
    out_ref[columns:reach, :] = -change[columns:] - later[columns:reach]
    out_ref[reach:, :] = -later[reach:]


def response_kernel(
    half, own_ref, got_ref, up_ref, local_ref, factor_ref, straddle_ref,
    base_ref, high_ref, low_ref,
):
    columns = base_ref.shape[0]
    reach = columns + half
    first_rows = slice(3 * half, 3 * half + columns)
    first = stack(own_ref[first_rows, :], own_ref[0:half, :])
    offset = product(first, up_ref[columns:, :])
    summed = stack(
        own_ref[3 * half + columns :, :] + offset[:columns] + up_ref[:columns, :],
        own_ref[half : 2 * half, :] + offset[columns:],
        own_ref[2 * half : 3 * half, :],
    )
    back = product(summed, factor_ref[1])
    change = product(back, straddle_ref[1][:, :half])
    local = beside(local_ref[:, :half] - change, local_ref[:, half:])
    base, middle, last = local[:columns], local[columns:reach], local[reach:]

    def store(at, value):
        high, low = split(value)
        high_ref[at * half : (at + 1) * half, :] = high
        low_ref[at * half : (at + 1) * half, :] = low

    @pl.when(core_now() != 0)
    def _():
        base_ref[...] = base
        store(0, middle)
        store(1, last)

    @pl.when(core_now() == 0)
    def _():
        middle_pair, last_pair = split(middle), split(last)
        zero = stack(got_ref[first_rows, :], got_ref[0:half, :])
        one = stack(got_ref[3 * half + columns :, :], got_ref[half : 3 * half, :])
        after_zero = product(zero, middle_pair)
        after_one = product(one, last_pair)
        base_ref[...] = base + after_zero[:columns] + after_one[:columns]
        store(0, after_zero[columns:] + after_one[columns:reach])
        store(1, after_one[reach:])


def final_kernel(
    own_ref, got_ref, own_kept_ref, got_kept_ref, base_ref, high_ref, low_ref, out_ref
):
    last = chip_now() == 0

    def body(even_ref, odd_ref, even_kept_ref, odd_kept_ref):
        carry = jnp.where(
            last,
            stack(even_ref[...], odd_ref[...]),
            stack(even_kept_ref[...], odd_kept_ref[...]),
        )
        reply = high_ref[...], low_ref[...]
        out_ref[...] = jnp.transpose(base_ref[...] + product(carry, reply))

    @pl.when(core_now() == 0)
    def _():
        body(own_ref, got_ref, own_kept_ref, got_kept_ref)

    @pl.when(core_now() != 0)
    def _():
        body(got_ref, own_ref, got_kept_ref, own_kept_ref)


def call(body, outs, *operands, flops=0):
    space = pl.BlockSpec(memory_space=pltpu.VMEM)
    shapes = [
        shape if isinstance(shape, jax.ShapeDtypeStruct) else jax.ShapeDtypeStruct(shape, F32)
        for shape in outs
    ]
    moved = sum(4 * operand.size for operand in operands) + sum(4 * shape.size for shape in shapes)
    return pl.pallas_call(
        body,
        out_shape=shapes,
        in_specs=[space] * len(operands),
        out_specs=[space] * len(shapes),
        compiler_params=pltpu.CompilerParams(vmem_limit_bytes=VMEM_GRANT),
        cost_estimate=pl.CostEstimate(flops=flops, bytes_accessed=moved, transcendentals=0),
    )(*operands)


def swap_route(count, step):
    power = count & (count - 1) == 0
    return [(i ^ step if power else (i + step) % count, i) for i in range(count)]


def passed(value, step):
    count = lax.axis_size("col")
    return lax.ppermute(value, "col", swap_route(count, step))


def gathered(straddle, own, early, late):
    count = lax.axis_size("col")
    if count == 4:
        near, side = passed(straddle, 1), passed(straddle, 2)
        near_late, side_early = passed(late, 1), passed(early, 2)
        far_early, far_late = passed(side[0:1], 1), passed(near[1:2], 2)
        near_early, side_late = passed(early, 1), passed(late, 2)
        first = [own, near, side, far_early, far_late]
        first_layout = [(0, 0), (1, 0), (2, 0), (3, 0), (3, 1)]
        second = [early, late, near_early, near_late, side_early, side_late]
        second += [passed(side_early, 1), passed(near_late, 2)]
        second_layout = [(step, sweep) for step in range(4) for sweep in range(2)]
        return first, first_layout, second, second_layout
    steps = range(1, count)
    first = [own] + [passed(straddle, step) for step in steps]
    second, second_layout = [early, late], [(0, 0), (0, 1)]
    for step in steps:
        for sweep, value in enumerate((early, late)):
            second.append(passed(value, step))
            second_layout.append((step, sweep))
    return first, [(step, 0) for step in range(count)], second, second_layout


def hop_routes(chips):
    routes = []
    for round_at in range(1, chips):
        pairs = {}
        for chip in range(chips - 2 + round_at % 2, 0, -2):
            pairs[chip], pairs[chip - 1] = chip - 1, chip
        route = []
        for chip in range(chips):
            for core in range(2):
                route.append((2 * chip + core, 2 * pairs[chip] + core if chip in pairs else 2 * chip + 1 - core))
        routes.append(route)
    return routes


def on_device(eigenvectors, aligned_vectors, straddle_vectors):
    aligned = jnp.swapaxes(aligned_vectors, 1, 2)
    straddle = jnp.swapaxes(straddle_vectors, 1, 2)
    sweeps, width, span = aligned.shape
    half = span // 2
    columns = eigenvectors.shape[1]
    part = columns // 2
    rows = lax.axis_size("row")
    chips = rows // 2
    unit = 2 * half * half * half * 3
    message = (half + PAD + columns, half)
    reach = columns + half
    half_pairs = lambda count: [jax.ShapeDtypeStruct((count, half, half), BF16)] * 2

    count = lax.axis_size("col")
    shard = (sweeps, width, span)
    current, own, early, late = call(
        first_kernel, [(columns, span), shard, (1,) + shard[1:], (1,) + shard[1:]],
        eigenvectors, straddle, aligned,
    )
    first, first_layout, second, second_layout = gathered(straddle, own, early, late)
    wide_straddle, inner, outer = call(
        functools.partial(gram_kernel, first_layout, count, half),
        [(sweeps, half, span), message, message],
        *first, current, flops=5 * unit,
    )
    inside_route = [(i, i ^ 1) for i in range(rows)]
    outside_route = [(i, i + 1) for i in range(1, rows - 1, 2)]
    outside_route += [(target, source) for source, target in outside_route]
    outer_got = lax.ppermute(outer, "row", outside_route)
    inner_got = lax.ppermute(inner, "row", inside_route)
    straddle_high, straddle_low, raw = call(
        functools.partial(between_kernel, half),
        half_pairs(2) + [(3, columns, half)],
        current, wide_straddle, flops=4 * unit,
    )
    wide_aligned, high, low, seen = call(
        functools.partial(aligned_kernel, second_layout, count, half),
        [(sweeps, half, span)] + half_pairs(11) + [(2, columns, half)],
        *second, current, wide_straddle, flops=40 * unit,
    )
    step, up, state, sight, factor, _ = call(
        functools.partial(local_kernel, columns, half),
        [
            (3 * half + 2 * columns, half), (reach, half), (reach, 3 * half), (reach, half),
            (3, half, half), (2, 2, half, half),
        ],
        inner, inner_got, outer, outer_got, high, low, seen,
        straddle_high, straddle_low, raw, flops=40 * unit,
    )
    step_got = lax.ppermute(step, "row", inside_route)
    up_got = lax.ppermute(up, "row", [(i, i + 1) for i in range(rows - 1)])
    (start,) = call(
        functools.partial(start_kernel, half), [(part, span)], step, step_got, flops=2 * unit
    )
    chain_high, chain_low = call(
        functools.partial(chain_kernel, half), half_pairs(3), step, step_got,
        flops=4 * unit,
    )
    (local,) = call(
        functools.partial(sweep_kernel, half), [(reach + half, span)],
        current, up, state, sight, factor, high, low, wide_straddle, wide_aligned,
        flops=20 * unit,
    )
    base, *reply = call(
        functools.partial(response_kernel, half),
        [(columns, span)] + [jax.ShapeDtypeStruct((span, span), BF16)] * 2,
        step, step_got, up_got, local, factor, wide_straddle, flops=20 * unit,
    )
    carry, got, kept = start, jnp.zeros_like(start), jnp.zeros_like(start)
    for hop, route in enumerate(hop_routes(chips), 1):
        got = lax.ppermute(carry, "row", route)
        if hop < chips - 1:
            carry, kept = call(
                functools.partial(hop_kernel, half, chips - 1 - hop),
                [(part, span), (part, span)],
                start, chain_high, chain_low, got, kept, flops=unit,
            )
    other_kept = lax.ppermute(kept, "row", inside_route)
    other = lax.ppermute(got, "row", inside_route)
    (result,) = call(
        final_kernel, [(span, columns)], got, other, kept, other_kept, base, *reply,
        flops=4 * unit,
    )
    return result


def solution(mesh):
    placed = (P("row", "col"), P(None, "row", "col"), P(None, "row", "col"))

    return jax.shard_map(
        on_device, mesh=mesh, in_specs=placed, out_specs=P("row", "col"), check_vma=False
    )
```

time: 77.1 us -> 61 us (0.79)
  waiting for transfers between devices: 35.7 us -> 11 us
  starting transfers between devices: 18.3 us -> 26.8 us
  local copies, waits for them, and re-layouts: 1.99 us -> 2.88 us
  Pallas kernels: 20.8 us -> 20 us
    ppermute x9 -> x14, waiting for transfers between devices: 34.1 us -> 8.69 us  [the longest x10 4.81 us: passed(): return lax.ppermute(value, 'col', swap_route(count, step))]
    ppermute x9 -> x14, starting transfers between devices: 12 us -> 21.8 us  [the longest x10 12.7 us: passed(): return lax.ppermute(value, 'col', swap_route(count, step))]
    ppermute x1, starting transfers between devices: 3.7 us -> 0.67 us  [on_device(): outer_got = lax.ppermute(outer, 'row', outside_route)]
    ppermute x1, starting transfers between devices: 0.07 us -> 2.35 us  [on_device(): step_got = lax.ppermute(step, 'row', inside_route)]
    ppermute x1, waiting for transfers between devices: 0.23 us -> 2.29 us  [on_device(): step_got = lax.ppermute(step, 'row', inside_route)]
    ppermute x1, waiting for transfers between devices: 1.35 us -> 0.01 us  [on_device(): other = lax.ppermute(got, 'row', inside_route)]
    unnamed x8 -> x6, local copies, waits for them, and re-layouts: 1.91 us -> 2.85 us
    pallas_call x8 -> x12, Pallas kernels: 20.8 us -> 20 us  [call(): pl.pallas_call(body, out_shape=shapes, in_specs=[space] * len(operands),...]
  transfers between devices with their start and end apart: 14 -> 19, of which waited for: 10 -> 8; matrix products, arithmetic and copies ran while one was open for 0% -> 0% of each run, Pallas kernels for 9% -> 20%
where the time goes in v2:
time: 61 us; the launch traced here: 60.8 us
  starting transfers between devices  26.8 us (44%)
  Pallas kernels  20 us (33%)
  waiting for transfers between devices  11 us (18%)
  local copies, waits for them, and re-layouts  2.88 us (5%)
    pallas_call x12, Pallas kernels, call(): pl.pallas_call(body, out_shape=shapes, in_specs=[space] * len(operands),...  20 us
    ppermute x10, starting transfers between devices, passed(): return lax.ppermute(value, 'col', swap_route(count, step))  12.7 us
    ppermute x3, starting transfers between devices, on_device(): got = lax.ppermute(carry, 'row', route)  8.42 us
    ppermute x10, waiting for transfers between devices, passed(): return lax.ppermute(value, 'col', swap_route(count, step))  4.81 us
    ppermute x3, waiting for transfers between devices, on_device(): got = lax.ppermute(carry, 'row', route)  3.88 us
    unnamed x6, local copies, waits for them, and re-layouts  2.85 us
    ppermute x1, starting transfers between devices, on_device(): step_got = lax.ppermute(step, 'row', inside_route)  2.35 us
    ppermute x1, waiting for transfers between devices, on_device(): step_got = lax.ppermute(step, 'row', inside_route)  2.29 us
  transfers between devices with their start and end apart: 19, of which 8 were waited for; matrix products, arithmetic and copies ran while one was open for 0% of the time, Pallas kernels for 20%

profile of v2, /device:TPU:0, one launch (start us, length us, event | category | flops | bytes accessed | tf_op | source)
XLA Modules:
  0.0 60.8 jit_solution(1620137095381268452)
XLA Ops:
  0.0 3.0 %collective-permute-start.1 = (f32[2,64,512]{2,1,0:T(8,128)}, f32[2,64,512]{2,1,0:T(8,128)S(1)}, u32[]{:S(2)}, u32[]{:S(2)}) collective-permute-start(f32[2,64,512]{2,1,0:T(8,128)} %bitcast.3), channel_id=1, source_target_pairs={{2,0},{3,1},{0,2},{1,3},{6,4},{7,5},{4,6},{5,7},{10,8},{11,9},{8,1... | collective-permute-start | bytes 786440 | tf_op jit(solution)/shard_map/ppermute | solution.py:508
  3.0 1.5 %collective-permute-start = (f32[2,64,512]{2,1,0:T(8,128)}, f32[2,64,512]{2,1,0:T(8,128)S(1)}, u32[]{:S(2)}, u32[]{:S(2)}) collective-permute-start(f32[2,64,512]{2,1,0:T(8,128)} %bitcast.4), channel_id=1, source_target_pairs={{1,0},{0,1},{3,2},{2,3},{5,4},{4,5},{7,6},{6,7},{9,8},{8,9},{11,10... | collective-permute-start | bytes 786440 | tf_op jit(solution)/shard_map/ppermute | solution.py:508
  4.5 0.9 %copy-done = f32[512,128]{1,0:T(8,128)S(1)} copy-done((f32[512,128]{1,0:T(8,128)S(1)}, f32[512,128]{1,0:T(8,128)}, u32[]{:S(2)}) %copy-start) | copy-done | bytes 262168
  5.4 0.9 %copy-done.1 = f32[2,512,64]{1,2,0:T(8,128)S(1)} copy-done((f32[2,512,64]{1,2,0:T(8,128)S(1)}, f32[2,512,64]{1,2,0:T(8,128)}, u32[]{:S(2)}) %copy-start.1) | copy-done | bytes 262168
  6.4 0.9 %copy-done.2 = f32[2,512,64]{1,2,0:T(8,128)S(1)} copy-done((f32[2,512,64]{1,2,0:T(8,128)S(1)}, f32[2,512,64]{1,2,0:T(8,128)}, u32[]{:S(2)}) %copy-start.2) | copy-done | bytes 262168
  8.2 1.9 %collective-permute-done.1.refs_2_ = f32[2,64,512]{2,1,0:T(8,128)S(1)} collective-permute-done((f32[2,64,512]{2,1,0:T(8,128)}, f32[2,64,512]{2,1,0:T(8,128)S(1)}, u32[]{:S(2)}, u32[]{:S(2)}) %collective-permute-start.1) | collective-permute-done | bytes 262176 | tf_op jit(solution)/shard_map/ppermute | solution.py:508
  10.0 2.4 %collective-permute-start.2 = (f32[1,64,512]{2,1,0:T(8,128)S(1)}, f32[1,64,512]{2,1,0:T(8,128)S(1)}, u32[]{:S(2)}, u32[]{:S(2)}) collective-permute-start(f32[1,64,512]{2,1,0:T(8,128)S(1)} %slice.8), channel_id=1, source_target_pairs={{1,0},{0,1},{3,2},{2,3},{5,4},{4,5},{7,6},{6,7},{9,8},{8,9},{11,10... | collective-permute-start | bytes 393224 | tf_op jit(solution)/shard_map/ppermute | solution.py:508
  12.4 1.6 %collective-permute-start.3 = (f32[1,64,512]{2,1,0:T(8,128)S(1)}, f32[1,64,512]{2,1,0:T(8,128)S(1)}, u32[]{:S(2)}, u32[]{:S(2)}) collective-permute-start(f32[1,64,512]{2,1,0:T(8,128)S(1)} %slice.9), channel_id=1, source_target_pairs={{2,0},{3,1},{0,2},{1,3},{6,4},{7,5},{4,6},{5,7},{10,8},{11,9},{8,1... | collective-permute-start | bytes 393224 | tf_op jit(solution)/shard_map/ppermute | solution.py:508
  14.6 1.4 %collective-permute-start.9 = (f32[1,64,512]{2,1,0:T(8,128)S(1)}, f32[1,64,512]{2,1,0:T(8,128)S(1)}, u32[]{:S(2)}, u32[]{:S(2)}) collective-permute-start(f32[1,64,512]{2,1,0:T(8,128)S(1)} %get-tuple-element.38.refs_1_), channel_id=1, source_target_pairs={{2,0},{3,1},{0,2},{1,3},{6,4},{7,5},{4,6},{5,7},{10,8},{11,9},{8,1... | collective-permute-start | bytes 393224 | tf_op jit(solution)/shard_map/ppermute | solution.py:508
  16.0 0.7 %collective-permute-start.10 = (f32[1,64,512]{2,1,0:T(8,128)S(1)}, f32[1,64,512]{2,1,0:T(8,128)S(1)}, u32[]{:S(2)}, u32[]{:S(2)}) collective-permute-start(f32[1,64,512]{2,1,0:T(8,128)S(1)} %collective-permute-done.8.refs_4_), channel_id=1, source_target_pairs={{1,0},{0,1},{3,2},{2,3},{5,4},{4,5},{7,6},{6,7},{9,8},{8,9},{11,10... | collective-permute-start | bytes 393224 | tf_op jit(solution)/shard_map/ppermute | solution.py:508
  16.7 1.2 %collective-permute-done.2.refs_3_ = f32[1,64,512]{2,1,0:T(8,128)S(1)} collective-permute-done((f32[1,64,512]{2,1,0:T(8,128)S(1)}, f32[1,64,512]{2,1,0:T(8,128)S(1)}, u32[]{:S(2)}, u32[]{:S(2)}) %collective-permute-start.2) | collective-permute-done | bytes 131104 | tf_op jit(solution)/shard_map/ppermute | solution.py:508
  17.9 0.9 %collective-permute-start.11 = (f32[1,64,512]{2,1,0:T(8,128)S(1)}, f32[1,64,512]{2,1,0:T(8,128)S(1)}, u32[]{:S(2)}, u32[]{:S(2)}) collective-permute-start(f32[1,64,512]{2,1,0:T(8,128)S(1)} %collective-permute-done.7.refs_3_), channel_id=1, source_target_pairs={{2,0},{3,1},{0,2},{1,3},{6,4},{7,5},{4,6},{5,7},{10,8},{11,9},{8,1... | collective-permute-start | bytes 393224 | tf_op jit(solution)/shard_map/ppermute | solution.py:508
  18.8 0.8 %shard_map.38 = (f32[2,256,512]{2,1,0:T(8,128)S(1)}, f32[392,256]{1,0:T(8,128)S(1)}, f32[392,256]{1,0:T(8,128)S(1)}) custom-call(f32[2,64,512]{2,1,0:T(8,128)S(1)} %get-tuple-element.33.refs_0_, f32[2,64,512]{2,1,0:T(8,128)S(1)} %collective-permute-done.refs_1_, f32[2,64,512]{2,1,0:T(8,128)S(1)} %collective-permute-done.1.refs_2_, ...), custom_call_target="tpu_custom_call" | custom-call | flops 503316480 | bytes 3162112 | tf_op jit(solution)/shard_map/pallas_call | solution.py:491
  19.8 1.0 %collective-permute-done.6.refs_2_ = f32[1,64,512]{2,1,0:T(8,128)S(1)} collective-permute-done((f32[1,64,512]{2,1,0:T(8,128)S(1)}, f32[1,64,512]{2,1,0:T(8,128)S(1)}, u32[]{:S(2)}, u32[]{:S(2)}) %collective-permute-start.6) | collective-permute-done | bytes 131104 | tf_op jit(solution)/shard_map/ppermute | solution.py:508
  20.7 0.7 %collective-permute-start.5 = (f32[392,256]{1,0:T(8,128)S(1)}, f32[392,256]{1,0:T(8,128)S(1)}, u32[]{:S(2)}, u32[]{:S(2)}) collective-permute-start(f32[392,256]{1,0:T(8,128)S(1)} %get-tuple-element.36.outer_ref), channel_id=1, source_target_pairs={{4,8},{12,16},{20,24},{8,4},{16,12},{24,20},{5,9},{13,17},{21,25},... | collective-permute-start | bytes 1204232 | tf_op jit(solution)/shard_map/ppermute | solution.py:577
  21.4 0.7 %shard_map.40 = (bf16[2,256,256]{2,1,0:T(8,128)(2,1)S(1)}, bf16[2,256,256]{2,1,0:T(8,128)(2,1)S(1)}, f32[3,128,256]{2,1,0:T(8,128)S(1)}) custom-call(f32[128,512]{1,0:T(8,128)S(1)} %get-tuple-element.34.refs_5_.refs_8_.current_ref, f32[2,256,512]{2,1,0:T(8,128)S(1)} %get-tuple-element.39.refs_9_.straddle_ref), custom_call_target="tpu_custom_call" | custom-call | flops 402653184 | bytes 2752512 | tf_op jit(solution)/shard_map/pallas_call | solution.py:491
  22.2 0.7 %collective-permute-done.11.refs_7_ = f32[1,64,512]{2,1,0:T(8,128)S(1)} collective-permute-done((f32[1,64,512]{2,1,0:T(8,128)S(1)}, f32[1,64,512]{2,1,0:T(8,128)S(1)}, u32[]{:S(2)}, u32[]{:S(2)}) %collective-permute-start.11) | collective-permute-done | bytes 131104 | tf_op jit(solution)/shard_map/ppermute | solution.py:508
  22.9 4.7 %shard_map.39 = (f32[2,256,512]{2,1,0:T(8,128)S(1)}, bf16[11,256,256]{2,1,0:T(8,128)(2,1)S(1)}, bf16[11,256,256]{2,1,0:T(8,128)(2,1)S(1)}, f32[2,128,256]{2,1,0:T(8,128)S(1)}) custom-call(f32[1,64,512]{2,1,0:T(8,128)S(1)} %get-tuple-element.37.refs_0_, f32[1,64,512]{2,1,0:T(8,128)S(1)} %get-tuple-element.38.refs_1_, ...), custom_call_target="tpu_custom_call" | custom-call | flops 4026531840 | bytes 9437184 | tf_op jit(solution)/shard_map/pallas_call | solution.py:491
  27.6 6.2 %shard_map.41 = (f32[1024,256]{1,0:T(8,128)S(1)}, f32[384,256]{1,0:T(8,128)S(1)}, f32[384,768]{1,0:T(8,128)S(1)}, f32[384,256]{1,0:T(8,128)S(1)}, f32[3,256,256]...) custom-call(f32[392,256]{1,0:T(8,128)S(1)} %get-tuple-element.35.inner_ref, ...), custom_call_target="tpu_custom_call" | custom-call | flops 4026531840 | bytes 13926400 | tf_op jit(solution)/shard_map/pallas_call | solution.py:491
  33.8 2.4 %collective-permute-start.12 = (f32[1024,256]{1,0:T(8,128)S(1)}, f32[1024,256]{1,0:T(8,128)S(1)}, u32[]{:S(2)}, u32[]{:S(2)}) collective-permute-start(f32[1024,256]{1,0:T(8,128)S(1)} %get-tuple-element.46.own_ref), channel_id=1, source_target_pairs={{0,4},{4,0},{8,12},{12,8},{16,20},{20,16},{24,28},{28,24},{1,5},{5... | collective-permute-start | bytes 3145736 | tf_op jit(solution)/shard_map/ppermute | solution.py:598
  36.1 2.3 %collective-permute-done.12.got_ref = f32[1024,256]{1,0:T(8,128)S(1)} collective-permute-done((f32[1024,256]{1,0:T(8,128)S(1)}, f32[1024,256]{1,0:T(8,128)S(1)}, u32[]{:S(2)}, u32[]{:S(2)}) %collective-permute-start.12) | collective-permute-done | bytes 1048608 | tf_op jit(solution)/shard_map/ppermute | solution.py:598
  38.7 2.1 %collective-permute-start.13 = (f32[64,512]{1,0:T(8,128)S(1)}, f32[64,512]{1,0:T(8,128)S(1)}, u32[]{:S(2)}, u32[]{:S(2)}) collective-permute-start(f32[64,512]{1,0:T(8,128)S(1)} %shard_map.42.start_ref), channel_id=1, source_target_pairs={{0,8},{4,12},{8,0},{12,4},{16,24},{20,28},{24,16},{28,20},{1,9},{5... | collective-permute-start | bytes 393224 | tf_op jit(solution)/shard_map/ppermute | solution.py:619
  40.8 1.8 %collective-permute-start.18 = (f32[384,256]{1,0:T(8,128)S(1)}, f32[384,256]{1,0:T(8,128)S(1)}, u32[]{:S(2)}, u32[]{:S(2)}) collective-permute-start(f32[384,256]{1,0:T(8,128)S(1)} %get-tuple-element.53.up_ref), channel_id=1, source_target_pairs={{0,4},{4,8},{8,12},{12,16},{16,20},{20,24},{24,28},{1,5},{5,9},{9,... | collective-permute-start | bytes 1179656 | tf_op jit(solution)/shard_map/ppermute | solution.py:599
  42.6 0.8 %shard_map.43 = (bf16[3,256,256]{2,1,0:T(8,128)(2,1)S(1)}, bf16[3,256,256]{2,1,0:T(8,128)(2,1)S(1)}) custom-call(f32[1024,256]{1,0:T(8,128)S(1)} %get-tuple-element.46.own_ref, f32[1024,256]{1,0:T(8,128)S(1)} %collective-permute-done.12.got_ref), custom_call_target="tpu_custom_call" | custom-call | flops 402653184 | bytes 3670016 | tf_op jit(solution)/shard_map/pallas_call | solution.py:491
  43.4 1.2 %collective-permute-done.13.got_ref = f32[64,512]{1,0:T(8,128)S(1)} collective-permute-done((f32[64,512]{1,0:T(8,128)S(1)}, f32[64,512]{1,0:T(8,128)S(1)}, u32[]{:S(2)}, u32[]{:S(2)}) %collective-permute-start.13) | collective-permute-done | bytes 131104 | tf_op jit(solution)/shard_map/ppermute | solution.py:619
  45.0 1.3 %collective-permute-done.14.got_ref = f32[64,512]{1,0:T(8,128)S(1)} collective-permute-done((f32[64,512]{1,0:T(8,128)S(1)}, f32[64,512]{1,0:T(8,128)S(1)}, u32[]{:S(2)}, u32[]{:S(2)}) %collective-permute-start.14) | collective-permute-done | bytes 131104 | tf_op jit(solution)/shard_map/ppermute | solution.py:619
  46.7 6.3 %collective-permute-start.15 = (f32[64,512]{1,0:T(8,128)S(1)}, f32[64,512]{1,0:T(8,128)S(1)}, u32[]{:S(2)}, u32[]{:S(2)}) collective-permute-start(f32[64,512]{1,0:T(8,128)S(1)} %get-tuple-element.51), channel_id=1, source_target_pairs={{0,8},{4,12},{8,0},{12,4},{16,24},{20,28},{24,16},{28,20},{1,9},{5... | collective-permute-start | bytes 393224 | tf_op jit(solution)/shard_map/ppermute | solution.py:619
  53.0 2.1 %shard_map.46.local_ref = f32[640,512]{1,0:T(8,128)S(1)} custom-call(f32[128,512]{1,0:T(8,128)S(1)} %get-tuple-element.34.refs_5_.refs_8_.current_ref, f32[384,256]{1,0:T(8,128)S(1)} %get-tuple-element.53.up_ref, f32[384,768]{1,0:T(8,128)S(1)} %get-tuple-element.54.state_ref, f32[384,256]{1,0:T(8,128)S(1)} %get-tuple-element.55.sight_ref, ...), custom_call_target="tpu_custom_call" | custom-call | flops 2013265920 | bytes 12189696 | tf_op jit(solution)/shard_map/pallas_call | solution.py:491
  55.1 0.7 %collective-permute-start.17 = (f32[64,512]{1,0:T(8,128)S(1)}, f32[64,512]{1,0:T(8,128)S(1)}, u32[]{:S(2)}, u32[]{:S(2)}) collective-permute-start(f32[64,512]{1,0:T(8,128)S(1)} %get-tuple-element.52.own_kept_ref), channel_id=1, source_target_pairs={{0,4},{4,0},{8,12},{12,8},{16,20},{20,16},{24,28},{28,24},{1,5},{5... | collective-permute-start | bytes 393224 | tf_op jit(solution)/shard_map/ppermute | solution.py:626
  55.8 1.3 %collective-permute-done.15.own_ref = f32[64,512]{1,0:T(8,128)S(1)} collective-permute-done((f32[64,512]{1,0:T(8,128)S(1)}, f32[64,512]{1,0:T(8,128)S(1)}, u32[]{:S(2)}, u32[]{:S(2)}) %collective-permute-start.15) | collective-permute-done | bytes 131104 | tf_op jit(solution)/shard_map/ppermute | solution.py:619
  57.3 2.3 %shard_map.47 = (f32[128,512]{1,0:T(8,128)S(1)}, bf16[512,512]{1,0:T(8,128)(2,1)S(1)}, bf16[512,512]{1,0:T(8,128)(2,1)S(1)}) custom-call(f32[1024,256]{1,0:T(8,128)S(1)} %get-tuple-element.46.own_ref, f32[1024,256]{1,0:T(8,128)S(1)} %collective-permute-done.12.got_ref, f32[384,256]{1,0:T(8,128)S(1)} %collective-permute-done.18.up_ref, ...), custom_call_target="tpu_custom_call" | custom-call | flops 2013265920 | bytes 7995392 | tf_op jit(solution)/shard_map/pallas_call | solution.py:491
  59.6 1.2 %shard_map.48 = f32[512,128]{1,0:T(8,128)} custom-call(f32[64,512]{1,0:T(8,128)S(1)} %collective-permute-done.15.own_ref, f32[64,512]{1,0:T(8,128)S(1)} %collective-permute-done.16.got_ref, f32[64,512]{1,0:T(8,128)S(1)} %get-tuple-element.52.own_kept_ref, f32[64,512]{1,0:T(8,128)S(1)} %collective-permute-done.17.got_kept_ref, ...), custom_call_target="tpu_custom_call" | custom-call | flops 402653184 | bytes 3145728 | tf_op jit(solution)/shard_map/pallas_call | solution.py:491
  (27 shorter events, 2.7 us)
Async XLA Ops:
  0.0 10.0 %collective-permute-start.1 = (f32[2,64,512]{2,1,0:T(8,128)}, f32[2,64,512]{2,1,0:T(8,128)S(1)}, u32[]{:S(2)}, u32[]{:S(2)}) collective-permute-start(f32[2,64,512]{2,1,0:T(8,128)} %bitcast.3), channel_id=1, source_target_pairs={{2,0},{3,1},{0,2},{1,3},{6,4},{7,5},{4,6},{5,7},{10,8},{11,9},{8,1... | collective-permute-start | bytes 786440 | tf_op jit(solution)/shard_map/ppermute | solution.py:508
  3.0 9.4 %collective-permute-start = (f32[2,64,512]{2,1,0:T(8,128)}, f32[2,64,512]{2,1,0:T(8,128)S(1)}, u32[]{:S(2)}, u32[]{:S(2)}) collective-permute-start(f32[2,64,512]{2,1,0:T(8,128)} %bitcast.4), channel_id=1, source_target_pairs={{1,0},{0,1},{3,2},{2,3},{5,4},{4,5},{7,6},{6,7},{9,8},{8,9},{11,10... | collective-permute-start | bytes 786440 | tf_op jit(solution)/shard_map/ppermute | solution.py:508
  4.5 0.9 %copy-start = (f32[512,128]{1,0:T(8,128)S(1)}, f32[512,128]{1,0:T(8,128)}, u32[]{:S(2)}) copy-start(f32[512,128]{1,0:T(8,128)} %matrix_ref.1) | copy-start | bytes 786436
  5.4 0.9 %copy-start.1 = (f32[2,512,64]{1,2,0:T(8,128)S(1)}, f32[2,512,64]{1,2,0:T(8,128)}, u32[]{:S(2)}) copy-start(f32[2,512,64]{1,2,0:T(8,128)} %param.4) | copy-start | bytes 786436
  6.4 0.9 %copy-start.2 = (f32[2,512,64]{1,2,0:T(8,128)S(1)}, f32[2,512,64]{1,2,0:T(8,128)}, u32[]{:S(2)}) copy-start(f32[2,512,64]{1,2,0:T(8,128)} %param.5) | copy-start | bytes 786436
  7.5 7.1 %collective-permute-start.8 = (f32[1,64,512]{2,1,0:T(8,128)S(1)}, f32[1,64,512]{2,1,0:T(8,128)S(1)}, u32[]{:S(2)}, u32[]{:S(2)}) collective-permute-start(f32[1,64,512]{2,1,0:T(8,128)S(1)} %get-tuple-element.37.refs_0_), channel_id=1, source_target_pairs={{2,0},{3,1},{0,2},{1,3},{6,4},{7,5},{4,6},{5,7},{10,8},{11,9},{8,1... | collective-permute-start | bytes 393224 | tf_op jit(solution)/shard_map/ppermute | solution.py:508
  8.0 7.9 %collective-permute-start.7 = (f32[1,64,512]{2,1,0:T(8,128)S(1)}, f32[1,64,512]{2,1,0:T(8,128)S(1)}, u32[]{:S(2)}, u32[]{:S(2)}) collective-permute-start(f32[1,64,512]{2,1,0:T(8,128)S(1)} %get-tuple-element.38.refs_1_), channel_id=1, source_target_pairs={{1,0},{0,1},{3,2},{2,3},{5,4},{4,5},{7,6},{6,7},{9,8},{8,9},{11,10... | collective-permute-start | bytes 393224 | tf_op jit(solution)/shard_map/ppermute | solution.py:508
  10.0 7.9 %collective-permute-start.2 = (f32[1,64,512]{2,1,0:T(8,128)S(1)}, f32[1,64,512]{2,1,0:T(8,128)S(1)}, u32[]{:S(2)}, u32[]{:S(2)}) collective-permute-start(f32[1,64,512]{2,1,0:T(8,128)S(1)} %slice.8), channel_id=1, source_target_pairs={{1,0},{0,1},{3,2},{2,3},{5,4},{4,5},{7,6},{6,7},{9,8},{8,9},{11,10... | collective-permute-start | bytes 393224 | tf_op jit(solution)/shard_map/ppermute | solution.py:508
  12.4 6.4 %collective-permute-start.3 = (f32[1,64,512]{2,1,0:T(8,128)S(1)}, f32[1,64,512]{2,1,0:T(8,128)S(1)}, u32[]{:S(2)}, u32[]{:S(2)}) collective-permute-start(f32[1,64,512]{2,1,0:T(8,128)S(1)} %slice.9), channel_id=1, source_target_pairs={{2,0},{3,1},{0,2},{1,3},{6,4},{7,5},{4,6},{5,7},{10,8},{11,9},{8,1... | collective-permute-start | bytes 393224 | tf_op jit(solution)/shard_map/ppermute | solution.py:508
  14.0 6.7 %collective-permute-start.6 = (f32[1,64,512]{2,1,0:T(8,128)S(1)}, f32[1,64,512]{2,1,0:T(8,128)S(1)}, u32[]{:S(2)}, u32[]{:S(2)}) collective-permute-start(f32[1,64,512]{2,1,0:T(8,128)S(1)} %get-tuple-element.37.refs_0_), channel_id=1, source_target_pairs={{1,0},{0,1},{3,2},{2,3},{5,4},{4,5},{7,6},{6,7},{9,8},{8,9},{11,10... | collective-permute-start | bytes 393224 | tf_op jit(solution)/shard_map/ppermute | solution.py:508
  14.6 7.6 %collective-permute-start.9 = (f32[1,64,512]{2,1,0:T(8,128)S(1)}, f32[1,64,512]{2,1,0:T(8,128)S(1)}, u32[]{:S(2)}, u32[]{:S(2)}) collective-permute-start(f32[1,64,512]{2,1,0:T(8,128)S(1)} %get-tuple-element.38.refs_1_), channel_id=1, source_target_pairs={{2,0},{3,1},{0,2},{1,3},{6,4},{7,5},{4,6},{5,7},{10,8},{11,9},{8,1... | collective-permute-start | bytes 393224 | tf_op jit(solution)/shard_map/ppermute | solution.py:508
  16.0 6.2 %collective-permute-start.10 = (f32[1,64,512]{2,1,0:T(8,128)S(1)}, f32[1,64,512]{2,1,0:T(8,128)S(1)}, u32[]{:S(2)}, u32[]{:S(2)}) collective-permute-start(f32[1,64,512]{2,1,0:T(8,128)S(1)} %collective-permute-done.8.refs_4_), channel_id=1, source_target_pairs={{1,0},{0,1},{3,2},{2,3},{5,4},{4,5},{7,6},{6,7},{9,8},{8,9},{11,10... | collective-permute-start | bytes 393224 | tf_op jit(solution)/shard_map/ppermute | solution.py:508
  17.9 5.0 %collective-permute-start.11 = (f32[1,64,512]{2,1,0:T(8,128)S(1)}, f32[1,64,512]{2,1,0:T(8,128)S(1)}, u32[]{:S(2)}, u32[]{:S(2)}) collective-permute-start(f32[1,64,512]{2,1,0:T(8,128)S(1)} %collective-permute-done.7.refs_3_), channel_id=1, source_target_pairs={{2,0},{3,1},{0,2},{1,3},{6,4},{7,5},{4,6},{5,7},{10,8},{11,9},{8,1... | collective-permute-start | bytes 393224 | tf_op jit(solution)/shard_map/ppermute | solution.py:508
  19.7 7.9 %collective-permute-start.4 = (f32[392,256]{1,0:T(8,128)S(1)}, f32[392,256]{1,0:T(8,128)S(1)}, u32[]{:S(2)}, u32[]{:S(2)}) collective-permute-start(f32[392,256]{1,0:T(8,128)S(1)} %get-tuple-element.35.inner_ref), channel_id=1, source_target_pairs={{0,4},{4,0},{8,12},{12,8},{16,20},{20,16},{24,28},{28,24},{1,5},{5... | collective-permute-start | bytes 1204232 | tf_op jit(solution)/shard_map/ppermute | solution.py:578
  20.7 6.8 %collective-permute-start.5 = (f32[392,256]{1,0:T(8,128)S(1)}, f32[392,256]{1,0:T(8,128)S(1)}, u32[]{:S(2)}, u32[]{:S(2)}) collective-permute-start(f32[392,256]{1,0:T(8,128)S(1)} %get-tuple-element.36.outer_ref), channel_id=1, source_target_pairs={{4,8},{12,16},{20,24},{8,4},{16,12},{24,20},{5,9},{13,17},{21,25},... | collective-permute-start | bytes 1204232 | tf_op jit(solution)/shard_map/ppermute | solution.py:577
  33.8 4.6 %collective-permute-start.12 = (f32[1024,256]{1,0:T(8,128)S(1)}, f32[1024,256]{1,0:T(8,128)S(1)}, u32[]{:S(2)}, u32[]{:S(2)}) collective-permute-start(f32[1024,256]{1,0:T(8,128)S(1)} %get-tuple-element.46.own_ref), channel_id=1, source_target_pairs={{0,4},{4,0},{8,12},{12,8},{16,20},{20,16},{24,28},{28,24},{1,5},{5... | collective-permute-start | bytes 3145736 | tf_op jit(solution)/shard_map/ppermute | solution.py:598
  38.7 5.8 %collective-permute-start.13 = (f32[64,512]{1,0:T(8,128)S(1)}, f32[64,512]{1,0:T(8,128)S(1)}, u32[]{:S(2)}, u32[]{:S(2)}) collective-permute-start(f32[64,512]{1,0:T(8,128)S(1)} %shard_map.42.start_ref), channel_id=1, source_target_pairs={{0,8},{4,12},{8,0},{12,4},{16,24},{20,28},{24,16},{28,20},{1,9},{5... | collective-permute-start | bytes 393224 | tf_op jit(solution)/shard_map/ppermute | solution.py:619
  40.8 16.5 %collective-permute-start.18 = (f32[384,256]{1,0:T(8,128)S(1)}, f32[384,256]{1,0:T(8,128)S(1)}, u32[]{:S(2)}, u32[]{:S(2)}) collective-permute-start(f32[384,256]{1,0:T(8,128)S(1)} %get-tuple-element.53.up_ref), channel_id=1, source_target_pairs={{0,4},{4,8},{8,12},{12,16},{16,20},{20,24},{24,28},{1,5},{5,9},{9,... | collective-permute-start | bytes 1179656 | tf_op jit(solution)/shard_map/ppermute | solution.py:599
  44.9 1.4 %collective-permute-start.14 = (f32[64,512]{1,0:T(8,128)S(1)}, f32[64,512]{1,0:T(8,128)S(1)}, u32[]{:S(2)}, u32[]{:S(2)}) collective-permute-start(f32[64,512]{1,0:T(8,128)S(1)} %get-tuple-element.49), channel_id=1, source_target_pairs={{0,4},{4,0},{8,16},{12,20},{16,8},{20,12},{24,28},{28,24},{1,5},{5... | collective-permute-start | bytes 393224 | tf_op jit(solution)/shard_map/ppermute | solution.py:619
  46.7 10.5 %collective-permute-start.15 = (f32[64,512]{1,0:T(8,128)S(1)}, f32[64,512]{1,0:T(8,128)S(1)}, u32[]{:S(2)}, u32[]{:S(2)}) collective-permute-start(f32[64,512]{1,0:T(8,128)S(1)} %get-tuple-element.51), channel_id=1, source_target_pairs={{0,8},{4,12},{8,0},{12,4},{16,24},{20,28},{24,16},{28,20},{1,9},{5... | collective-permute-start | bytes 393224 | tf_op jit(solution)/shard_map/ppermute | solution.py:619
  55.1 4.4 %collective-permute-start.17 = (f32[64,512]{1,0:T(8,128)S(1)}, f32[64,512]{1,0:T(8,128)S(1)}, u32[]{:S(2)}, u32[]{:S(2)}) collective-permute-start(f32[64,512]{1,0:T(8,128)S(1)} %get-tuple-element.52.own_kept_ref), channel_id=1, source_target_pairs={{0,4},{4,0},{8,12},{12,8},{16,20},{20,16},{24,28},{28,24},{1,5},{5... | collective-permute-start | bytes 393224 | tf_op jit(solution)/shard_map/ppermute | solution.py:626
  57.1 2.4 %collective-permute-start.16 = (f32[64,512]{1,0:T(8,128)S(1)}, f32[64,512]{1,0:T(8,128)S(1)}, u32[]{:S(2)}, u32[]{:S(2)}) collective-permute-start(f32[64,512]{1,0:T(8,128)S(1)} %collective-permute-done.15.own_ref), channel_id=1, source_target_pairs={{0,4},{4,0},{8,12},{12,8},{16,20},{20,16},{24,28},{28,24},{1,5},{5... | collective-permute-start | bytes 393224 | tf_op jit(solution)/shard_map/ppermute | solution.py:627
